TPU v7x, 512 devices: a whole 4x8x8 slice. The times are simulated.
512 devices in a mesh: ctx: 32 (over z, x_hi, core), head: 16 (over y, x_lo).
Axes of the slice: x: 4 (x_hi: 2, x_lo: 2; x = x_hi * 2 + x_lo), y: 8, z: 8, core: 2. Of those that a mesh axis runs over, the one named last changes fastest.
Arguments:
- tokens: bfloat16 [131072, 1024], P(('ctx', 'head')), may hold values from -11 to 11
- ln_gain: float32 [1024], replicated, may hold values from 0.1 to 1.9
- ln_bias: float32 [1024], replicated, may hold values from -3 to 3
- qkv_weight: bfloat16 [1024, 16, 192], P(None, 'head'), may hold values from -7 to 7
- out_weight: bfloat16 [1024, 1024], P('head'), may hold values from -0.75 to 0.75
- output_bias_vector: float32 [1024], replicated, may hold values from -3 to 3
- lengths: int32 [1024], replicated, may hold values from 1 to 512, 131072 in all
- pairs_dev: int32 [1024, 3], replicated, may hold values from 0 to 31, all different within a row; in each aligned block of 32 rows (0 to 31, 32 to 63, ...) at most 4 rows name the same one
- pairs_off: int32 [1024, 3], replicated, may hold values from 0 to 31
Outputs:
- attended_out: bfloat16 [131072, 1024], P(('ctx', 'head'))
Inputs may be any that keep to these rules, and one draw needn't show every extreme that they name: The lengths sum to 131072. `pairs_dev`: each row names 3 different ctx indices; within the rows of one ctx index's 32 query blocks no ctx index is named more than 4 times.
All inputs are finite; a program needn't handle non-finite values.
Results may differ from a plain program's by a relative error of at most 0.0065.
The roundings to bfloat16 on the way count: a program that leaves them out, or rounds other values in their place, can miss the bound.
Values may be sent and summed in bfloat16 or wider, within the bound.
No kernel may reach another device: no remote copies, remote signals or barrier semaphores. Data moves between devices by JAX's collectives and lax.ppermute only.
A program may use at most 64 MiB of HBM per device.

v0:
```python
import jax
import jax.numpy as jnp
from jax import lax
from jax.experimental import pallas as pl
from jax.experimental.pallas import tpu as pltpu
from jax.sharding import PartitionSpec as P


BLK = 128
RAND = 3
CAP = 4
EPS = 1e-05
NEG = float("-inf")
TN = (((0,), (1,)), ((), ()))


def ln_kernel(tok_ref, gain_ref, bias_ref, normt_ref, first_ref, last_ref):
    values = tok_ref[...].astype(jnp.float32)
    center = values - jnp.mean(values, axis=-1, keepdims=True)
    spread = jnp.mean(center * center, axis=-1, keepdims=True)
    normed = center * lax.rsqrt(spread + EPS) * gain_ref[...] + bias_ref[...]
    turned = jnp.transpose(normed).astype(jnp.bfloat16).reshape(normt_ref.shape)
    normt_ref[...] = turned
    first_ref[...] = turned[:, :, :BLK]
    last_ref[...] = turned[:, :, turned.shape[2] - BLK :]


def layer_norm(tokens, gain, bias, heads):
    rows, width = tokens.shape
    return pl.pallas_call(
        ln_kernel,
        out_shape=tuple(
            jax.ShapeDtypeStruct((heads, width // heads, cols), jnp.bfloat16)
            for cols in (rows, BLK, BLK)
        ),
        name="layer_norm",
    )(tokens, gain.reshape(1, width), bias.reshape(1, width))


def pick_kernel(ids_ref, cells_ref, out_ref):
    def step(slot, carry):
        block = ids_ref[slot]
        cols = pl.ds(pl.multiple_of((block % 2) * BLK, BLK), BLK)
        out_ref[slot] = cells_ref[block // 2, :, cols]
        return carry

    lax.fori_loop(0, out_ref.shape[0], step, 0, unroll=4)


def pick_blocks(ids, cells):
    return pl.pallas_call(
        pick_kernel,
        out_shape=jax.ShapeDtypeStruct((ids.shape[0], cells.shape[1], BLK), jnp.bfloat16),
        in_specs=[
            pl.BlockSpec(memory_space=pltpu.SMEM),
            pl.BlockSpec(memory_space=pltpu.VMEM),
        ],
        out_specs=pl.BlockSpec(memory_space=pltpu.VMEM),
        name="pick_blocks",
    )(ids, cells)


def place_kernel(pos_ref, slots_ref, shared_ref, out_ref):
    per_dev = out_ref.shape[2] // BLK - 1

    def step(dev, carry):
        for j in range(per_dev):
            out_ref[dev, :, j * BLK : (j + 1) * BLK] = slots_ref[pos_ref[dev * per_dev + j]]
        out_ref[dev, :, per_dev * BLK :] = shared_ref[...]
        return carry

    lax.fori_loop(0, out_ref.shape[0], step, 0)


def place_blocks(pos, slots, shared, heads):
    cols = (pos.shape[0] // heads + 1) * BLK
    return pl.pallas_call(
        place_kernel,
        out_shape=jax.ShapeDtypeStruct((heads, slots.shape[1], cols), jnp.bfloat16),
        in_specs=[
            pl.BlockSpec(memory_space=pltpu.SMEM),
            pl.BlockSpec(memory_space=pltpu.VMEM),
            pl.BlockSpec(memory_space=pltpu.VMEM),
        ],
        out_specs=pl.BlockSpec(memory_space=pltpu.VMEM),
        name="place_blocks",
    )(pos, slots, shared)


def both_heads(qt_pair):
    half = qt_pair.shape[0] // 2
    none = jnp.zeros((half, qt_pair.shape[1]), qt_pair.dtype)
    top = jnp.concatenate([qt_pair[:half], none], axis=1)
    return jnp.concatenate([top, jnp.concatenate([none, qt_pair[half:]], axis=1)], axis=0)


def own_halves(wide):
    half, cols = wide.shape[0] // 2, wide.shape[1] // 2
    return jnp.concatenate([wide[:half, :cols], wide[half:, cols:]], axis=0)


def spread_rows(row, half):
    cols = row.shape[1] // 2
    top = jnp.broadcast_to(row[:, :cols], (half, cols))
    return jnp.concatenate([top, jnp.broadcast_to(row[:, cols:], (half, cols))], axis=0)


def near_kernel(qt_ref, k_ref, vt_ref, mask_ref, acc_ref, top_ref, sum_ref):
    f32 = jnp.float32
    scores = []
    for b in range(2):
        q = both_heads(qt_ref[:, b * BLK : (b + 1) * BLK])
        keys = k_ref[b * BLK : (b + 3) * BLK, :]
        mask = mask_ref[b]
        s = jnp.dot(keys, q, preferred_element_type=f32)
        scores.append(s + jnp.concatenate([mask, mask], axis=1))
    for b, s in enumerate(scores):
        top = jnp.max(s, axis=0, keepdims=True)
        p = jnp.exp(s - top)
        total = jnp.sum(p, axis=0, keepdims=True)
        near = slice(b * BLK, (b + 3) * BLK)
        acc = jnp.dot(vt_ref[:, near], p.astype(jnp.bfloat16), preferred_element_type=f32)
        acc_ref[:, b * BLK : (b + 1) * BLK] = own_halves(acc)
        top_ref[0, b] = jnp.broadcast_to(top, top_ref.shape[2:])
        sum_ref[0, b] = jnp.broadcast_to(total, sum_ref.shape[2:])


def far_kernel(qt_ref, k_ref, vt_ref, acc_ref, top_ref, sum_ref, out_ref):
    f32 = jnp.float32
    spread = RAND * BLK
    shared = slice(2 * spread, 2 * spread + BLK)
    scores = []
    for b in range(2):
        q = both_heads(qt_ref[:, b * BLK : (b + 1) * BLK])
        keys = k_ref[b * spread : (b + 1) * spread, :]
        s = jnp.dot(keys, q, preferred_element_type=f32)
        scores.append((s, jnp.dot(k_ref[shared, :], q, preferred_element_type=f32)))
    for b, (s, g) in enumerate(scores):
        cols = slice(b * BLK, (b + 1) * BLK)
        far = slice(b * spread, (b + 1) * spread)
        old_top = top_ref[0, b, :1]
        top = jnp.maximum(jnp.max(s, axis=0, keepdims=True), old_top)
        top = jnp.maximum(jnp.max(g, axis=0, keepdims=True), top)
        p = jnp.exp(s - top)
        pg = jnp.exp(g - top)
        scale = jnp.exp(old_top - top)
        total = jnp.sum(p, axis=0, keepdims=True) + sum_ref[0, b, :1] * scale
        total += jnp.sum(pg, axis=0, keepdims=True)
        acc = jnp.dot(vt_ref[:, far], p.astype(jnp.bfloat16), preferred_element_type=f32)
        acc += jnp.dot(vt_ref[:, shared], pg.astype(jnp.bfloat16), preferred_element_type=f32)
        half = acc.shape[0] // 2
        acc = own_halves(acc) + acc_ref[:, cols] * spread_rows(scale, half)
        out_ref[:, cols] = (acc / spread_rows(total, half)).astype(jnp.bfloat16)


def pair_specs(rows, keys):
    tall = pl.BlockSpec((BLK, rows), lambda i: (i, 0))
    k_spec = pl.BlockSpec((keys, BLK), lambda i: (0, i))
    vt_spec = pl.BlockSpec((BLK, keys), lambda i: (i, 0))
    row = pl.BlockSpec((1, rows // BLK, 8, 2 * BLK), lambda i: (i, 0, 0, 0))
    return tall, k_spec, vt_spec, row


def near_attention(qt, k, vt, mask):
    width, rows = qt.shape
    pairs = width // BLK
    tall, k_spec, vt_spec, row = pair_specs(rows, k.shape[0])
    stat = jax.ShapeDtypeStruct((pairs, rows // BLK, 8, 2 * BLK), jnp.float32)
    return pl.pallas_call(
        near_kernel,
        out_shape=(jax.ShapeDtypeStruct((width, rows), jnp.float32), stat, stat),
        grid=(pairs,),
        in_specs=[tall, k_spec, vt_spec, pl.BlockSpec(mask.shape, lambda i: (0, 0, 0))],
        out_specs=(tall, row, row),
        name="near_attention",
    )(qt, k, vt, mask)


def far_attention(qt, k, vt, parts):
    width, rows = qt.shape
    tall, k_spec, vt_spec, row = pair_specs(rows, k.shape[0])
    return pl.pallas_call(
        far_kernel,
        out_shape=jax.ShapeDtypeStruct((width, rows), jnp.bfloat16),
        grid=(width // BLK,),
        in_specs=[tall, k_spec, vt_spec, tall, row, row],
        out_specs=tall,
        name="far_attention",
    )(qt, k, vt, *parts)


def run_copies(copies):
    for copy in copies:
        copy.start()
    for copy in copies:
        copy.wait()


def piece_kernel(core_ref, wt_ref, out_w_ref, piece_ref, sems):
    rows, cols = wt_ref.shape[0], piece_ref.shape[1]
    mine = pl.ds(pl.multiple_of(core_ref[0] * cols, cols), cols)
    run_copies(
        [
            pltpu.make_async_copy(wt_ref.at[:, mine], piece_ref.at[:rows], sems.at[0]),
            pltpu.make_async_copy(out_w_ref.at[:, mine], piece_ref.at[rows:], sems.at[1]),
        ]
    )


def any_specs(count):
    return [pl.BlockSpec(memory_space=pl.ANY)] * count


def own_piece(core, wt, out_w):
    rows = wt.shape[0] + out_w.shape[0]
    return pl.pallas_call(
        piece_kernel,
        out_shape=jax.ShapeDtypeStruct((rows, wt.shape[1] // 2), jnp.bfloat16),
        in_specs=[pl.BlockSpec(memory_space=pltpu.SMEM)] + any_specs(2),
        out_specs=pl.BlockSpec(memory_space=pltpu.VMEM),
        scratch_shapes=[pltpu.SemaphoreType.DMA((2,))],
        name="own_piece",
    )(core, wt, out_w)


def assemble_kernel(core_ref, *refs):
    sems = refs[-1]
    outs, parts = refs[-5:-1], refs[:-5]
    heads, hd, width = outs[0].shape
    cols = width // 2
    copies, head = [], 0
    for n, part in enumerate(parts):
        side = core_ref[0] if head < heads else 1 - core_ref[0]
        into_cols = pl.ds(pl.multiple_of(side * cols, cols), cols)
        count = part.shape[0]
        into_heads = pl.ds(head % heads, count)
        head += count
        for k, out in enumerate(outs):
            copies.append(
                pltpu.make_async_copy(
                    part.at[:, pl.ds(k * hd, hd)],
                    out.at[into_heads, :, into_cols],
                    sems.at[n * len(outs) + k],
                )
            )
    run_copies(copies)


def assemble(core, parts, heads, hd):
    cols = parts[0].shape[2]
    one = jax.ShapeDtypeStruct((heads, hd, 2 * cols), jnp.bfloat16)
    return pl.pallas_call(
        assemble_kernel,
        out_shape=(one,) * 4,
        in_specs=[pl.BlockSpec(memory_space=pltpu.SMEM)] + any_specs(len(parts)),
        out_specs=(pl.BlockSpec(memory_space=pltpu.VMEM),) * 4,
        scratch_shapes=[pltpu.SemaphoreType.DMA((4 * len(parts),))],
        name="assemble",
    )(core, *parts)


def tied(value, *others):
    return lax.optimization_barrier((value,) + others)[0]


def swap(value, bits, devices):
    return lax.ppermute(value, ("ctx", "head"), [(i, i ^ bits) for i in range(devices)])


def exchange_plan(pairs_dev, pairs_off, ctx_count, ctx_index, lower):
    pair_count = lower.shape[0]
    all_dev = pairs_dev.reshape(ctx_count, pair_count)
    all_off = pairs_off.reshape(ctx_count, pair_count)
    own = all_dev == ctx_index
    rank = jnp.sum((own[:, None, :] & lower[None]).astype(jnp.int32), axis=2)
    slot = jnp.arange(CAP, dtype=jnp.int32)
    chosen = own[:, None, :] & (rank[:, None, :] == slot[None, :, None])
    send = jnp.sum(jnp.where(chosen, all_off[:, None, :], 0), axis=2)
    send = send.reshape(-1)
    own_dev = lax.dynamic_index_in_dim(all_dev, ctx_index, 0, keepdims=False)
    earlier = (own_dev[:, None] == own_dev[None, :]) & lower
    take = own_dev * CAP + jnp.sum(earlier.astype(jnp.int32), axis=1)
    return send, take


def window_mask(lengths, first_pos, doc_tokens, rows):
    line_end = jnp.cumsum(lengths)
    positions = first_pos - BLK + jnp.arange(rows + 2 * BLK, dtype=jnp.int32)
    line = jnp.sum((line_end[None, :] <= positions[:, None]).astype(jnp.int32), axis=1)
    inside = (positions >= 0) & (positions < doc_tokens)
    line = jnp.where(inside, line, -1)
    masks = []
    for b in range(rows // BLK):
        keys = line[b * BLK : (b + 3) * BLK]
        queries = line[(b + 1) * BLK : (b + 2) * BLK]
        masks.append(jnp.where(keys[:, None] == queries[None, :], 0.0, NEG))
    return jnp.stack(masks).astype(jnp.float32)


def per_device(
    tokens, ln_gain, ln_bias, qkv_weight, out_weight, out_bias, lengths, pairs_dev, pairs_off
):
    ctx_count = lax.axis_size("ctx")
    heads = lax.axis_size("head")
    devices = ctx_count * heads
    ctx_index = lax.axis_index("ctx")
    head_index = lax.axis_index("head")
    rows, width = tokens.shape
    hd = width // heads

    wt = jnp.transpose(qkv_weight[:, 0, :])
    core = (ctx_index % 2).astype(jnp.int32).reshape(1)
    place = ctx_index * heads + head_index

    normed_t, first, last = layer_norm(tokens, ln_gain, ln_bias, heads)
    cells = lax.all_to_all(normed_t, "head", split_axis=0, concat_axis=0, tiled=True)

    own = own_piece(core, wt, out_weight)
    along_y = [list(range(first_x, heads, 2)) for first_x in range(2)]
    column = lax.all_gather(own, "head", axis_index_groups=along_y)

    both = ("ctx", "head")
    right = [(i, i + 1) for i in range(devices - 1)]
    left = [(i + 1, i) for i in range(devices - 1)]
    before = lax.ppermute(last, both, right)
    after = lax.ppermute(first, both, left)

    pair_count = (heads * rows // BLK) * RAND
    order = jnp.arange(pair_count, dtype=jnp.int32)
    lower = order[None, :] < order[:, None]
    send, take = exchange_plan(pairs_dev, pairs_off, ctx_count, ctx_index, lower)
    outgoing = pick_blocks(tied(send, own, before, after), cells)
    outgoing = outgoing.reshape(ctx_count, CAP * hd, BLK)
    slots = lax.all_to_all(outgoing, "ctx", split_axis=0, concat_axis=0, tiled=True)
    slots = slots.reshape(ctx_count * CAP, hd, BLK)

    half = column.shape[0] // 2
    mine = [column, swap(column[:half], 1, devices), swap(column[half:], 2 * heads + 1, devices)]
    other = [swap(part, heads, devices) for part in mine]
    shared = jnp.where(ctx_index == 0, cells[0, :, :BLK], 0).astype(jnp.bfloat16)
    reach = 1
    while reach < ctx_count:
        hop = [(i, i + reach) for i in range(reach)]
        shared = shared + lax.ppermute(shared, "ctx", hop)
        reach *= 2
    placed = place_blocks(tied(take, column), slots, shared, heads)
    far = lax.all_to_all(placed, "head", split_axis=0, concat_axis=0, tiled=True)
    far = far.reshape(width, far.shape[2])

    near = jnp.concatenate([before, normed_t, after], axis=2)
    near = near.reshape(width, near.shape[2])

    mask = window_mask(lengths, place * rows, devices * rows, rows)

    f32 = jnp.float32
    bf16 = jnp.bfloat16
    weights = assemble(core, mine + other, heads, hd)
    w_q, w_k, w_v, w_o = (w.reshape(width, width) for w in weights)
    own_t = normed_t.reshape(width, rows)
    qt = jnp.dot(w_q, own_t, preferred_element_type=f32).astype(bf16)
    qt = (qt.astype(f32) * hd**-0.5).astype(bf16)
    k_near = lax.dot_general(near, w_k, TN, preferred_element_type=f32).astype(bf16)
    vt_near = jnp.dot(w_v, near, preferred_element_type=f32).astype(bf16)
    parts = near_attention(qt, k_near, vt_near, mask)
    k_far = lax.dot_general(far, w_k, TN, preferred_element_type=f32).astype(bf16)
    vt_far = jnp.dot(w_v, far, preferred_element_type=f32).astype(bf16)
    attended = far_attention(qt, k_far, vt_far, parts)
    projected = lax.dot_general(
        attended, w_o, (((0,), (0,)), ((), ())), preferred_element_type=f32
    )
    return (projected + out_bias).astype(bf16)


def solution(mesh):
    in_specs = (
        P(("ctx", "head"), None),
        P(),
        P(),
        P(None, "head", None),
        P("head", None),
        P(),
        P(),
        P(),
        P(),
    )

    return jax.shard_map(
        per_device,
        mesh=mesh,
        in_specs=in_specs,
        out_specs=P(("ctx", "head"), None),
        check_vma=False,
    )
```

profile of v0, /device:TPU:7, one launch (start us, length us, event | category | flops | bytes accessed | tf_op | source)
XLA Modules:
  0.0 225.0 jit_solution(5672278928059613308)
XLA Ops:
  6.5 2.4 %layer_norm.1 = (bf16[16,64,256]{2,1,0:T(8,128)(2,1)}, bf16[16,64,128]{2,1,0:T(8,128)(2,1)}, bf16[16,64,128]{2,1,0:T(8,128)(2,1)}) custom-call(bf16[256,1024]{1,0:T(8,128)(2,1)} %tok_ref.1, f32[1,1024]{1,0:T(1,128)} %bitcast.50, f32[1,1024]{1,0:T(1,128)} %bitcast.51), custom_call_target="tpu_custom_call" | custom-call | tf_op jit(solution)/shard_map/layer_norm/pallas_call | solution.py:30
  9.0 8.0 %all-to-all-start = ((bf16[16,64,256]{2,1,0:T(8,128)(2,1)}), bf16[16,64,256]{2,1,0:T(8,128)(2,1)S(1)}, u32[]{:S(2)}, u32[]{:S(2)}) async-start(bf16[16,64,256]{2,1,0:T(8,128)(2,1)} %get-tuple-element.18), calls=%async_computation | async-start | bytes 1048576 | tf_op jit(solution)/shard_map/all_to_all | solution.py:316
  17.0 3.1 %collective-permute-start.5 = (bf16[16,64,128]{2,1,0:T(8,128)(2,1)}, bf16[16,64,128]{2,1,0:T(8,128)(2,1)S(1)}, u32[]{:S(2)}, u32[]{:S(2)}) collective-permute-start(bf16[16,64,128]{2,1,0:T(8,128)(2,1)} %get-tuple-element.20), channel_id=1, source_target_pairs={{0,1},{1,2},{2,3},{3,4},{4,5},{5,6},{6,7},{7,8},{8,9},{9,10},{10,1... | collective-permute-start | bytes 786440 | tf_op jit(solution)/shard_map/ppermute | solution.py:325
  20.1 2.2 collective-permute-start.6
  22.3 0.9 copy.12
  23.2 0.3 reshape.192
  23.6 0.2 copy.13
  23.8 0.3 broadcast_in_dim.48
  24.1 0.6 convert_reduce_fusion.1
  24.7 0.1 select_reduce_fusion
  24.8 0.1 copy.14
  24.9 0.6 reshape.193.ids_ref
  25.5 1.7 own_piece.1
  27.2 6.3 %collective-permute-done.5 = bf16[16,64,128]{2,1,0:T(8,128)(2,1)S(1)} collective-permute-done((bf16[16,64,128]{2,1,0:T(8,128)(2,1)}, bf16[16,64,128]{2,1,0:T(8,128)(2,1)S(1)}, u32[]{:S(2)}, u32[]{:S(2)}) %collective-permute-start.5) | collective-permute-done | bytes 262176 | tf_op jit(solution)/shard_map/ppermute | solution.py:325
  33.5 2.8 %collective-permute-done.6 = bf16[16,64,128]{2,1,0:T(8,128)(2,1)S(1)} collective-permute-done((bf16[16,64,128]{2,1,0:T(8,128)(2,1)}, bf16[16,64,128]{2,1,0:T(8,128)(2,1)S(1)}, u32[]{:S(2)}, u32[]{:S(2)}) %collective-permute-start.6) | collective-permute-done | bytes 262176 | tf_op jit(solution)/shard_map/ppermute | solution.py:326
  36.3 0.8 copy-done.2
  37.1 3.7 %pick_blocks.1 = bf16[128,64,128]{2,1,0:T(8,128)(2,1)} custom-call(s32[128]{0:T(128)} %reshape.193.ids_ref, bf16[16,64,256]{2,1,0:T(8,128)(2,1)} %copy-done.2), custom_call_target="tpu_custom_call" | custom-call | tf_op jit(solution)/shard_map/pick_blocks/pallas_call | solution.py:51
  40.8 14.9 %all-to-all-start.1 = ((bf16[32,256,128]{2,1,0:T(8,128)(2,1)}), bf16[32,256,128]{2,1,0:T(8,128)(2,1)S(1)}, u32[]{:S(2)}, u32[]{:S(2)}) async-start(bf16[32,256,128]{2,1,0:T(8,128)(2,1)} %bitcast.42), calls=%async_computation.1 | async-start | bytes 4194304 | tf_op jit(solution)/shard_map/all_to_all | solution.py:334
  55.6 0.0 all-gather.3.cloned.1.call-start
  55.7 0.7 all-gather.3.cloned.1.call-update
  56.4 0.7 fusion.5
  57.1 0.7 collective-permute-start.7
  57.8 0.7 fusion.21
  58.5 1.3 collective-permute-start.8
  59.8 5.1 %collective-permute-done.8 = bf16[64,128]{1,0:T(8,128)(2,1)S(1)} collective-permute-done((bf16[64,128]{1,0:T(8,128)(2,1)S(1)}, bf16[64,128]{1,0:T(8,128)(2,1)S(1)}, u32[]{:S(2)}, u32[]{:S(2)}) %collective-permute-start.8) | collective-permute-done | bytes 16416 | tf_op jit(solution)/shard_map/ppermute | solution.py:344
  64.9 1.3 collective-permute-start.9
  66.2 33.3 %collective-permute-done.9 = bf16[64,128]{1,0:T(8,128)(2,1)S(1)} collective-permute-done((bf16[64,128]{1,0:T(8,128)(2,1)S(1)}, bf16[64,128]{1,0:T(8,128)(2,1)S(1)}, u32[]{:S(2)}, u32[]{:S(2)}) %collective-permute-start.9) | collective-permute-done | bytes 16416 | tf_op jit(solution)/shard_map/ppermute | solution.py:344
  99.5 1.3 collective-permute-start.10
  100.8 0.2 convert_reduce_fusion.2
  101.0 0.7 collective-permute-done.10
  101.7 1.3 collective-permute-start.11
  103.0 0.6 multiply_add_fusion.pos_ref
  103.5 0.3 collective-permute-done.11
  103.8 0.6 add.55.shared_ref
  104.4 1.5 all-to-all-done.1
  105.9 1.3 copy-done
  107.3 3.3 %place_blocks.1 = bf16[16,64,896]{2,1,0:T(8,128)(2,1)} custom-call(s32[96]{0:T(128)} %multiply_add_fusion.pos_ref, bf16[128,64,128]{2,1,0:T(8,128)(2,1)} %bitcast.41, bf16[64,128]{1,0:T(8,128)(2,1)} %add.55.shared_ref), custom_call_target="tpu_custom_call" | custom-call | tf_op jit(solution)/shard_map/place_blocks/pallas_call | solution.py:77
  110.6 9.5 %all-to-all-start.2 = ((bf16[16,64,896]{2,1,0:T(8,128)(2,1)}), bf16[16,64,896]{2,1,0:T(8,128)(2,1)}, u32[]{:S(2)}, u32[]{:S(2)}) async-start(bf16[16,64,896]{2,1,0:T(8,128)(2,1)} %place_blocks.1), calls=%async_computation.2 | async-start | bytes 3670016 | tf_op jit(solution)/shard_map/all_to_all | solution.py:347
  120.0 0.0 copy-start.8
  120.0 1.5 fusion.6
  121.5 2.0 collective-permute-start
  123.6 2.5 %collective-permute-start.1 = (bf16[4,256,512]{2,1,0:T(8,128)(2,1)}, bf16[4,256,512]{2,1,0:T(8,128)(2,1)}, u32[]{:S(2)}, u32[]{:S(2)}) collective-permute-start(bf16[4,256,512]{2,1,0:T(8,128)(2,1)} %bitcast.5), channel_id=1, source_target_pairs={{0,33},{1,32},{2,35},{3,34},{4,37},{5,36},{6,39},{7,38},{8,41},{9,... | collective-permute-start | bytes 3145736 | tf_op jit(solution)/shard_map/ppermute | solution.py:267
  126.1 3.7 %collective-permute-start.2 = (bf16[8,256,512]{2,1,0:T(8,128)(2,1)S(1)}, bf16[8,256,512]{2,1,0:T(8,128)(2,1)}, u32[]{:S(2)}, u32[]{:S(2)}) collective-permute-start(bf16[8,256,512]{2,1,0:T(8,128)(2,1)S(1)} %bitcast.44), channel_id=1, source_target_pairs={{0,16},{1,17},{2,18},{3,19},{4,20},{5,21},{6,22},{7,23},{8,24},{9,... | collective-permute-start | bytes 6291464 | tf_op jit(solution)/shard_map/ppermute | solution.py:267
  129.9 0.3 reduce-window.9
  130.1 0.1 slice.31
  130.3 0.1 slice_reduce_fusion
  130.4 0.1 add_bitcast_fusion
  130.4 0.4 convert_reduce_fusion
  130.8 33.4 %collective-permute-done.refs_1_ = bf16[4,256,512]{2,1,0:T(8,128)(2,1)} collective-permute-done((bf16[4,256,512]{2,1,0:T(8,128)(2,1)}, bf16[4,256,512]{2,1,0:T(8,128)(2,1)}, u32[]{:S(2)}, u32[]{:S(2)}) %collective-permute-start) | collective-permute-done | bytes 1048608 | tf_op jit(solution)/shard_map/ppermute | solution.py:267
  164.2 4.2 %collective-permute-start.3 = (bf16[4,256,512]{2,1,0:T(8,128)(2,1)}, bf16[4,256,512]{2,1,0:T(8,128)(2,1)}, u32[]{:S(2)}, u32[]{:S(2)}) collective-permute-start(bf16[4,256,512]{2,1,0:T(8,128)(2,1)} %collective-permute-done.refs_1_), channel_id=1, source_target_pairs={{0,16},{1,17},{2,18},{3,19},{4,20},{5,21},{6,22},{7,23},{8,24},{9,... | collective-permute-start | bytes 3145736 | tf_op jit(solution)/shard_map/ppermute | solution.py:267
  168.4 2.1 collective-permute-start.4
  170.6 0.2 compare_select_fusion
  170.7 0.8 pad_maximum_fusion.1.mask_ref
  171.5 1.1 pad_maximum_fusion
  172.6 0.7 collective-permute-done.4.refs_5_
  173.3 6.8 %assemble.1 = (bf16[16,64,1024]{2,1,0:T(8,128)(2,1)}, bf16[16,64,1024]{2,1,0:T(8,128)(2,1)}, bf16[16,64,1024]{2,1,0:T(8,128)(2,1)}, bf16[16,64,1024]{2,1,0:T(8,128)(2,1)}) custom-call(s32[1]{0:T(128)} %bitcast.core_ref, bf16[8,256,512]{2,1,0:T(8,128)(2,1)} %bitcast.43, bf16[4,256,512]{2,1,0:T(8,128)(2,1)} %collective-permute-done.refs_1_, ...), custom_call_target="tpu_custom_call" | custom-call | tf_op jit(solution)/shard_map/assemble/pallas_call | solution.py:252
  180.1 3.2 %fusion.2.qt_ref = bf16[1024,256]{1,0:T(8,128)(2,1)} fusion(bf16[1024,1024]{1,0:T(8,128)(2,1)} %bitcast.57, bf16[1024,256]{1,0:T(8,128)(2,1)S(1)} %bitcast.46), kind=kOutput, calls=%fused_computation.10 | convolution fusion | flops 537919488 | bytes 3145728 | tf_op jit(solution)/shard_map/dot_general | solution.py:360
  183.4 2.3 %convolution_convert_fusion.2.vt_ref = bf16[1024,512]{1,0:T(8,128)(2,1)} fusion(bf16[1024,1024]{1,0:T(8,128)(2,1)S(1)} %bitcast.56, bf16[1024,512]{1,0:T(8,128)(2,1)S(1)} %bitcast.47), kind=kOutput, calls=%fused_computation.4 | convolution fusion | flops 1074266112 | bytes 4194304 | tf_op jit(solution)/shard_map/dot_general | solution.py:363
  185.7 2.3 %convolution_convert_fusion.3.k_ref = bf16[512,1024]{1,0:T(8,128)(2,1)} fusion(bf16[1024,512]{1,0:T(8,128)(2,1)S(1)} %bitcast.48, bf16[1024,1024]{1,0:T(8,128)(2,1)S(1)} %bitcast.53), kind=kOutput, calls=%fused_computation.5 | convolution fusion | flops 1074266112 | bytes 4194304 | tf_op jit(solution)/shard_map/dot_general | solution.py:362
  188.0 8.2 %near_attention.1 = (f32[1024,256]{1,0:T(8,128)}, f32[8,2,8,256]{3,2,1,0:T(8,128)}, f32[8,2,8,256]{3,2,1,0:T(8,128)}) custom-call(bf16[1024,256]{1,0:T(8,128)(2,1)} %fusion.2.qt_ref, bf16[512,1024]{1,0:T(8,128)(2,1)} %convolution_convert_fusion.3.k_ref, bf16[1024,512]{1,0:T(8,128)(2,1)} %convolution_convert_fusion.2.vt_ref, ...), custom_call_target="tpu_custom_call" | custom-call | tf_op jit(solution)/shard_map/near_attention/pallas_call | solution.py:169
  196.1 5.7 %convolution_convert_fusion.vt_ref = bf16[1024,896]{1,0:T(8,128)(2,1)} fusion(bf16[1024,1024]{1,0:T(8,128)(2,1)} %bitcast.55, bf16[1024,896]{1,0:T(8,128)(2,1)} %bitcast.14), kind=kOutput, calls=%fused_computation.1 | convolution fusion | flops 1879965696 | bytes 5767168 | tf_op jit(solution)/shard_map/dot_general | solution.py:366
  201.8 4.9 %convolution_convert_fusion.1.k_ref = bf16[896,1024]{1,0:T(8,128)(2,1)} fusion(bf16[1024,896]{1,0:T(8,128)(2,1)} %bitcast.14, bf16[1024,1024]{1,0:T(8,128)(2,1)S(1)} %bitcast.54), kind=kOutput, calls=%fused_computation.2 | convolution fusion | flops 1879965696 | bytes 5767168 | tf_op jit(solution)/shard_map/dot_general | solution.py:365
  206.7 8.9 %far_attention.1 = bf16[1024,256]{1,0:T(8,128)(2,1)} custom-call(bf16[1024,256]{1,0:T(8,128)(2,1)} %fusion.2.qt_ref, bf16[896,1024]{1,0:T(8,128)(2,1)} %convolution_convert_fusion.1.k_ref, bf16[1024,896]{1,0:T(8,128)(2,1)} %convolution_convert_fusion.vt_ref, f32[1024,256]{1,0:T(8,128)} %get-tuple-element.25.acc_ref, ...), custom_call_target="tpu_custom_call" | custom-call | tf_op jit(solution)/shard_map/far_attention/pallas_call | solution.py:182
  215.6 2.6 %fusion.3 = bf16[256,1024]{1,0:T(8,128)(2,1)} fusion(bf16[1024,256]{1,0:T(8,128)(2,1)} %far_attention.1, bf16[1024,1024]{1,0:T(8,128)(2,1)S(1)} %bitcast.45, f32[1024]{0:T(1024)S(1)} %copy-done.6), kind=kOutput, calls=%fused_computation.11 | convolution fusion | flops 537395200 | bytes 3149824 | tf_op jit(solution)/shard_map/dot_general | solution.py:368
  (37 shorter events, 0.2 us)
Async XLA Ops:
  6.5 17.0 %copy-start.7 = (s32[1024,3]{0,1:T(4,128)S(1)}, s32[1024,3]{0,1:T(4,128)}, u32[]{:S(2)}) copy-start(s32[1024,3]{0,1:T(4,128)} %param.17) | copy-start | bytes 36868
  9.0 27.3 %all-to-all-start = ((bf16[16,64,256]{2,1,0:T(8,128)(2,1)}), bf16[16,64,256]{2,1,0:T(8,128)(2,1)S(1)}, u32[]{:S(2)}, u32[]{:S(2)}) async-start(bf16[16,64,256]{2,1,0:T(8,128)(2,1)} %get-tuple-element.18), calls=%async_computation | async-start | bytes 1048576 | tf_op jit(solution)/shard_map/all_to_all | solution.py:316
  17.0 16.5 %collective-permute-start.5 = (bf16[16,64,128]{2,1,0:T(8,128)(2,1)}, bf16[16,64,128]{2,1,0:T(8,128)(2,1)S(1)}, u32[]{:S(2)}, u32[]{:S(2)}) collective-permute-start(bf16[16,64,128]{2,1,0:T(8,128)(2,1)} %get-tuple-element.20), channel_id=1, source_target_pairs={{0,1},{1,2},{2,3},{3,4},{4,5},{5,6},{6,7},{7,8},{8,9},{9,10},{10,1... | collective-permute-start | bytes 786440 | tf_op jit(solution)/shard_map/ppermute | solution.py:325
  20.1 16.2 %collective-permute-start.6 = (bf16[16,64,128]{2,1,0:T(8,128)(2,1)}, bf16[16,64,128]{2,1,0:T(8,128)(2,1)S(1)}, u32[]{:S(2)}, u32[]{:S(2)}) collective-permute-start(bf16[16,64,128]{2,1,0:T(8,128)(2,1)} %get-tuple-element.21), channel_id=1, source_target_pairs={{1,0},{2,1},{3,2},{4,3},{5,4},{6,5},{7,6},{8,7},{9,8},{10,9},{11,1... | collective-permute-start | bytes 786440 | tf_op jit(solution)/shard_map/ppermute | solution.py:326
  36.3 0.8 copy-start.2
  40.8 65.1 %all-to-all-start.1 = ((bf16[32,256,128]{2,1,0:T(8,128)(2,1)}), bf16[32,256,128]{2,1,0:T(8,128)(2,1)S(1)}, u32[]{:S(2)}, u32[]{:S(2)}) async-start(bf16[32,256,128]{2,1,0:T(8,128)(2,1)} %bitcast.42), calls=%async_computation.1 | async-start | bytes 4194304 | tf_op jit(solution)/shard_map/all_to_all | solution.py:334
  55.6 48.8 %all-gather.3.cloned.1.call-start = ((), (), s32[]{:S(2)}) async-start(), calls=%async_computation.3 | async-start | bytes 2359296 | tf_op jit(solution)/shard_map/all_gather | solution.py:320
  57.1 0.7 collective-permute-start.7
  58.5 6.4 %collective-permute-start.8 = (bf16[64,128]{1,0:T(8,128)(2,1)S(1)}, bf16[64,128]{1,0:T(8,128)(2,1)S(1)}, u32[]{:S(2)}, u32[]{:S(2)}) collective-permute-start(bf16[64,128]{1,0:T(8,128)(2,1)S(1)} %fusion.21), channel_id=1, source_target_pairs={{0,32},{16,48},{1,33},{17,49},{2,34},{18,50},{3,35},{19,51},{4,36}... | collective-permute-start | bytes 49160 | tf_op jit(solution)/shard_map/ppermute | solution.py:344
  64.9 34.6 %collective-permute-start.9 = (bf16[64,128]{1,0:T(8,128)(2,1)S(1)}, bf16[64,128]{1,0:T(8,128)(2,1)S(1)}, u32[]{:S(2)}, u32[]{:S(2)}) collective-permute-start(bf16[64,128]{1,0:T(8,128)(2,1)S(1)} %add.52), channel_id=1, source_target_pairs={{0,64},{16,80},{32,96},{48,112},{1,65},{17,81},{33,97},{49,113},{2... | collective-permute-start | bytes 49160 | tf_op jit(solution)/shard_map/ppermute | solution.py:344
  99.5 2.1 collective-permute-start.10
  101.7 2.1 collective-permute-start.11
  105.9 1.3 copy-start
  110.5 9.5 %copy-start.1 = (bf16[2048,512]{1,0:T(8,128)(2,1)S(1)}, bf16[2048,512]{1,0:T(8,128)(2,1)}, u32[]{:S(2)}) copy-start(bf16[2048,512]{1,0:T(8,128)(2,1)} %all-gather.3.cloned.1.call-done) | copy-start | bytes 6291460
  110.6 85.6 %all-to-all-start.2 = ((bf16[16,64,896]{2,1,0:T(8,128)(2,1)}), bf16[16,64,896]{2,1,0:T(8,128)(2,1)}, u32[]{:S(2)}, u32[]{:S(2)}) async-start(bf16[16,64,896]{2,1,0:T(8,128)(2,1)} %place_blocks.1), calls=%async_computation.2 | async-start | bytes 3670016 | tf_op jit(solution)/shard_map/all_to_all | solution.py:347
  120.0 9.8 %copy-start.8 = (s32[1024]{0:T(1024)S(1)}, s32[1024]{0:T(1024)}, u32[]{:S(2)}) copy-start(s32[1024]{0:T(1024)} %param.15) | copy-start | bytes 12292
  120.0 51.5 %copy-start.4 = (bf16[16,64,256]{2,1,0:T(8,128)(2,1)S(1)}, bf16[16,64,256]{2,1,0:T(8,128)(2,1)}, u32[]{:S(2)}) copy-start(bf16[16,64,256]{2,1,0:T(8,128)(2,1)} %get-tuple-element.18) | copy-start | bytes 1572868
  121.5 42.6 %collective-permute-start = (bf16[4,256,512]{2,1,0:T(8,128)(2,1)}, bf16[4,256,512]{2,1,0:T(8,128)(2,1)}, u32[]{:S(2)}, u32[]{:S(2)}) collective-permute-start(bf16[4,256,512]{2,1,0:T(8,128)(2,1)} %bitcast.4), channel_id=1, source_target_pairs={{0,1},{1,0},{2,3},{3,2},{4,5},{5,4},{6,7},{7,6},{8,9},{9,8},{10,11... | collective-permute-start | bytes 3145736 | tf_op jit(solution)/shard_map/ppermute | solution.py:267
  123.6 44.8 %collective-permute-start.1 = (bf16[4,256,512]{2,1,0:T(8,128)(2,1)}, bf16[4,256,512]{2,1,0:T(8,128)(2,1)}, u32[]{:S(2)}, u32[]{:S(2)}) collective-permute-start(bf16[4,256,512]{2,1,0:T(8,128)(2,1)} %bitcast.5), channel_id=1, source_target_pairs={{0,33},{1,32},{2,35},{3,34},{4,37},{5,36},{6,39},{7,38},{8,41},{9,... | collective-permute-start | bytes 3145736 | tf_op jit(solution)/shard_map/ppermute | solution.py:267
  126.1 47.2 %collective-permute-start.2 = (bf16[8,256,512]{2,1,0:T(8,128)(2,1)S(1)}, bf16[8,256,512]{2,1,0:T(8,128)(2,1)}, u32[]{:S(2)}, u32[]{:S(2)}) collective-permute-start(bf16[8,256,512]{2,1,0:T(8,128)(2,1)S(1)} %bitcast.44), channel_id=1, source_target_pairs={{0,16},{1,17},{2,18},{3,19},{4,20},{5,21},{6,22},{7,23},{8,24},{9,... | collective-permute-start | bytes 6291464 | tf_op jit(solution)/shard_map/ppermute | solution.py:267
  164.2 8.5 %collective-permute-start.3 = (bf16[4,256,512]{2,1,0:T(8,128)(2,1)}, bf16[4,256,512]{2,1,0:T(8,128)(2,1)}, u32[]{:S(2)}, u32[]{:S(2)}) collective-permute-start(bf16[4,256,512]{2,1,0:T(8,128)(2,1)} %collective-permute-done.refs_1_), channel_id=1, source_target_pairs={{0,16},{1,17},{2,18},{3,19},{4,20},{5,21},{6,22},{7,23},{8,24},{9,... | collective-permute-start | bytes 3145736 | tf_op jit(solution)/shard_map/ppermute | solution.py:267
  168.4 4.9 %collective-permute-start.4 = (bf16[4,256,512]{2,1,0:T(8,128)(2,1)}, bf16[4,256,512]{2,1,0:T(8,128)(2,1)}, u32[]{:S(2)}, u32[]{:S(2)}) collective-permute-start(bf16[4,256,512]{2,1,0:T(8,128)(2,1)} %collective-permute-done.1.refs_2_), channel_id=1, source_target_pairs={{0,16},{1,17},{2,18},{3,19},{4,20},{5,21},{6,22},{7,23},{8,24},{9,... | collective-permute-start | bytes 3145736 | tf_op jit(solution)/shard_map/ppermute | solution.py:267
  180.1 3.3 %copy-start.5 = (bf16[16,64,512]{2,1,0:T(8,128)(2,1)S(1)}, bf16[16,64,512]{2,1,0:T(8,128)(2,1)}, u32[]{:S(2)}) copy-start(bf16[16,64,512]{2,1,0:T(8,128)(2,1)} %pad_maximum_fusion) | copy-start | bytes 3145732
  180.1 3.3 %copy-start.10 = (bf16[16,64,1024]{2,1,0:T(8,128)(2,1)S(1)}, bf16[16,64,1024]{2,1,0:T(8,128)(2,1)}, u32[]{:S(2)}) copy-start(bf16[16,64,1024]{2,1,0:T(8,128)(2,1)} %get-tuple-element.24) | copy-start | bytes 6291460
  183.4 2.3 %copy-start.9 = (bf16[16,64,1024]{2,1,0:T(8,128)(2,1)S(1)}, bf16[16,64,1024]{2,1,0:T(8,128)(2,1)}, u32[]{:S(2)}) copy-start(bf16[16,64,1024]{2,1,0:T(8,128)(2,1)} %get-tuple-element.23) | copy-start | bytes 6291460
  206.7 8.9 %copy-start.3 = (bf16[16,64,1024]{2,1,0:T(8,128)(2,1)S(1)}, bf16[16,64,1024]{2,1,0:T(8,128)(2,1)}, u32[]{:S(2)}) copy-start(bf16[16,64,1024]{2,1,0:T(8,128)(2,1)} %get-tuple-element.28) | copy-start | bytes 6291460
  206.7 8.9 %copy-start.6 = (f32[1024]{0:T(1024)S(1)}, f32[1024]{0:T(1024)}, u32[]{:S(2)}) copy-start(f32[1024]{0:T(1024)} %param.14) | copy-start | bytes 12292
Sparse Core Ops, SparseCore 0:
  58.5 41.7 all-gather.2
where the time goes:
time: 226 us; the launch traced here: 225 us
  waiting for transfers between devices  84.6 us (37%)
  starting transfers between devices  58.1 us (26%)
  Pallas kernels  34.9 us (15%)
  matrix products  20.9 us (9%)
  between operations  13.7 us (6%)
  other arithmetic  6.41 us (3%)
  local copies, waits for them, and re-layouts  6.28 us (3%)
    ppermute x5, waiting for transfers between devices, per_device(): shared = shared + lax.ppermute(shared, 'ctx', hop)  39.4 us
    ppermute x5, waiting for transfers between devices, swap(): lax.ppermute(value, ('ctx', 'head'), [(i, i ^ bits) for i in range(device...  34 us
    all_to_all x1, starting transfers between devices, per_device(): lax.all_to_all(outgoing, 'ctx', split_axis=0, concat_axis=0, tiled=True)  14.9 us
    ppermute x5, starting transfers between devices, swap(): lax.ppermute(value, ('ctx', 'head'), [(i, i ^ bits) for i in range(device...  14.7 us
    all_to_all x1, starting transfers between devices, per_device(): lax.all_to_all(placed, 'head', split_axis=0, concat_axis=0, tiled=True)  9.46 us
    pallas_call x1, Pallas kernels, far_attention(): pl.pallas_call(far_kernel, out_shape=jax.ShapeDtypeStruct((width, rows),...  8.89 us
    pallas_call x1, Pallas kernels, near_attention(): pl.pallas_call(near_kernel, out_shape=(jax.ShapeDtypeStruct((width, rows)...  8.16 us
    all_to_all x1, starting transfers between devices, per_device(): lax.all_to_all(normed_t, 'head', split_axis=0, concat_axis=0, tiled=True)  8.01 us
  transfers between devices with their start and end apart: 16, of which 9 were waited for; matrix products, arithmetic and copies ran while one was open for 8% of the time, Pallas kernels for 7%

commit v1 on v0

--- a/solution.py
+++ b/solution.py
@@ -322,14 +322,14 @@
     both = ("ctx", "head")
     right = [(i, i + 1) for i in range(devices - 1)]
     left = [(i + 1, i) for i in range(devices - 1)]
-    before = lax.ppermute(last, both, right)
-    after = lax.ppermute(first, both, left)
+    before = lax.ppermute(tied(last, cells), both, right)
+    after = lax.ppermute(tied(first, cells), both, left)
 
     pair_count = (heads * rows // BLK) * RAND
     order = jnp.arange(pair_count, dtype=jnp.int32)
     lower = order[None, :] < order[:, None]
     send, take = exchange_plan(pairs_dev, pairs_off, ctx_count, ctx_index, lower)
-    outgoing = pick_blocks(tied(send, own, before, after), cells)
+    outgoing = pick_blocks(tied(send, own), cells)
     outgoing = outgoing.reshape(ctx_count, CAP * hd, BLK)
     slots = lax.all_to_all(outgoing, "ctx", split_axis=0, concat_axis=0, tiled=True)
     slots = slots.reshape(ctx_count * CAP, hd, BLK)
@@ -338,12 +338,17 @@
     mine = [column, swap(column[:half], 1, devices), swap(column[half:], 2 * heads + 1, devices)]
     other = [swap(part, heads, devices) for part in mine]
     shared = jnp.where(ctx_index == 0, cells[0, :, :BLK], 0).astype(jnp.bfloat16)
-    reach = 1
-    while reach < ctx_count:
+    group = 4
+    for reach in (1, 2):
         hop = [(i, i + reach) for i in range(reach)]
         shared = shared + lax.ppermute(shared, "ctx", hop)
-        reach *= 2
-    placed = place_blocks(tied(take, column), slots, shared, heads)
+    copies = [
+        lax.ppermute(shared, "ctx", [(i, i + reach) for i in range(group)])
+        for reach in range(group, ctx_count, group)
+    ]
+    for copy in copies:
+        shared = shared + copy
+    placed = place_blocks(tied(take, column, before, after), slots, shared, heads)
     far = lax.all_to_all(placed, "head", split_axis=0, concat_axis=0, tiled=True)
     far = far.reshape(width, far.shape[2])
 

time: 226 us -> 223 us (0.987)
  waiting for transfers between devices: 84.6 us -> 80.4 us
    ppermute x5 -> x2, waiting for transfers between devices: 39.4 us -> 5.07 us  [per_device(): shared = shared + lax.ppermute(shared, 'ctx', hop)]
    ppermute x2 -> x9, waiting for transfers between devices: 9.09 us -> 31.6 us  [the longest x7 29.6 us: per_device(): lax.ppermute(shared, 'ctx', [(i, i + reach) for i in range(group)])]
    all_to_all x1, waiting for transfers between devices: 0.01 us -> 9.37 us  [per_device(): lax.all_to_all(normed_t, 'head', split_axis=0, concat_axis=0, tiled=True)]
    ppermute x2 -> x9, starting transfers between devices: 5.27 us -> 13.8 us  [the longest x7 9.03 us: per_device(): lax.ppermute(shared, 'ctx', [(i, i + reach) for i in range(group)])]
    all_to_all x1, starting transfers between devices: 9.46 us -> 4.46 us  [per_device(): lax.all_to_all(placed, 'head', split_axis=0, concat_axis=0, tiled=True)]
    ppermute x5 -> x2, starting transfers between devices: 5.8 us -> 1.93 us  [per_device(): shared = shared + lax.ppermute(shared, 'ctx', hop)]
  transfers between devices with their start and end apart: 16 -> 20, of which waited for: 9 -> 7; matrix products, arithmetic and copies ran while one was open for 8% -> 8% of each run, Pallas kernels for 7% -> 8%
where the time goes in v1:
time: 223 us; the launch traced here: 221 us
  waiting for transfers between devices  80.4 us (36%)
  starting transfers between devices  58.7 us (26%)
  Pallas kernels  35 us (16%)
  matrix products  21 us (9%)
  between operations  13.8 us (6%)
  other arithmetic  6.39 us (3%)
  local copies, waits for them, and re-layouts  6.23 us (3%)
    ppermute x5, waiting for transfers between devices, swap(): lax.ppermute(value, ('ctx', 'head'), [(i, i ^ bits) for i in range(device...  33.6 us
    ppermute x7, waiting for transfers between devices, per_device(): lax.ppermute(shared, 'ctx', [(i, i + reach) for i in range(group)])  29.6 us
    all_to_all x1, starting transfers between devices, per_device(): lax.all_to_all(outgoing, 'ctx', split_axis=0, concat_axis=0, tiled=True)  15.4 us
    ppermute x5, starting transfers between devices, swap(): lax.ppermute(value, ('ctx', 'head'), [(i, i ^ bits) for i in range(device...  15.1 us
    all_to_all x1, waiting for transfers between devices, per_device(): lax.all_to_all(normed_t, 'head', split_axis=0, concat_axis=0, tiled=True)  9.37 us
    ppermute x7, starting transfers between devices, per_device(): lax.ppermute(shared, 'ctx', [(i, i + reach) for i in range(group)])  9.03 us
    pallas_call x1, Pallas kernels, far_attention(): pl.pallas_call(far_kernel, out_shape=jax.ShapeDtypeStruct((width, rows),...  8.89 us
    pallas_call x1, Pallas kernels, near_attention(): pl.pallas_call(near_kernel, out_shape=(jax.ShapeDtypeStruct((width, rows)...  8.18 us
  transfers between devices with their start and end apart: 20, of which 7 were waited for; matrix products, arithmetic and copies ran while one was open for 8% of the time, Pallas kernels for 8%

profile of v1, /device:TPU:7, one launch (start us, length us, event | category | flops | bytes accessed | tf_op | source)
XLA Modules:
  0.0 221.4 jit_solution(1952648847116917348)
XLA Ops:
  6.5 2.5 %layer_norm.1 = (bf16[16,64,256]{2,1,0:T(8,128)(2,1)}, bf16[16,64,128]{2,1,0:T(8,128)(2,1)}, bf16[16,64,128]{2,1,0:T(8,128)(2,1)}) custom-call(bf16[256,1024]{1,0:T(8,128)(2,1)} %tok_ref.1, f32[1,1024]{1,0:T(1,128)} %bitcast.50, f32[1,1024]{1,0:T(1,128)} %bitcast.51), custom_call_target="tpu_custom_call" | custom-call | tf_op jit(solution)/shard_map/layer_norm/pallas_call | solution.py:30
  9.0 8.0 %all-to-all-start = ((bf16[16,64,256]{2,1,0:T(8,128)(2,1)}), bf16[16,64,256]{2,1,0:T(8,128)(2,1)S(1)}, u32[]{:S(2)}, u32[]{:S(2)}) async-start(bf16[16,64,256]{2,1,0:T(8,128)(2,1)} %get-tuple-element.20), calls=%async_computation | async-start | bytes 1048576 | tf_op jit(solution)/shard_map/all_to_all | solution.py:316
  17.0 0.9 copy.12
  17.9 0.3 reshape.192
  18.2 0.2 copy.13
  18.5 0.3 broadcast_in_dim.48
  18.8 0.6 convert_reduce_fusion.1
  19.4 0.1 select_reduce_fusion
  19.5 0.1 copy.14
  19.6 0.6 reshape.193.ids_ref
  20.3 1.6 own_piece.1
  21.9 9.4 %all-to-all-done.cells_ref = bf16[16,64,256]{2,1,0:T(8,128)(2,1)S(1)} async-done(((bf16[16,64,256]{2,1,0:T(8,128)(2,1)}), bf16[16,64,256]{2,1,0:T(8,128)(2,1)S(1)}, u32[]{:S(2)}, u32[]{:S(2)}) %all-to-all-start) | async-done | bytes 524320 | tf_op jit(solution)/shard_map/all_to_all | solution.py:316
  31.3 0.8 copy-done.2
  32.1 3.7 %pick_blocks.1 = bf16[128,64,128]{2,1,0:T(8,128)(2,1)} custom-call(s32[128]{0:T(128)} %reshape.193.ids_ref, bf16[16,64,256]{2,1,0:T(8,128)(2,1)} %copy-done.2), custom_call_target="tpu_custom_call" | custom-call | tf_op jit(solution)/shard_map/pick_blocks/pallas_call | solution.py:51
  35.7 15.4 %all-to-all-start.1 = ((bf16[32,256,128]{2,1,0:T(8,128)(2,1)}), bf16[32,256,128]{2,1,0:T(8,128)(2,1)S(1)}, u32[]{:S(2)}, u32[]{:S(2)}) async-start(bf16[32,256,128]{2,1,0:T(8,128)(2,1)} %bitcast.42), calls=%async_computation.1 | async-start | bytes 4194304 | tf_op jit(solution)/shard_map/all_to_all | solution.py:334
  51.2 0.7 all-gather.3.cloned.1.call-update
  51.9 0.7 fusion.5
  52.6 0.7 collective-permute-start.7
  53.3 0.7 fusion.21
  54.0 1.3 collective-permute-start.8
  55.3 5.1 %collective-permute-done.8 = bf16[64,128]{1,0:T(8,128)(2,1)S(1)} collective-permute-done((bf16[64,128]{1,0:T(8,128)(2,1)S(1)}, bf16[64,128]{1,0:T(8,128)(2,1)S(1)}, u32[]{:S(2)}, u32[]{:S(2)}) %collective-permute-start.8) | collective-permute-done | bytes 16416 | tf_op jit(solution)/shard_map/ppermute | solution.py:344
  60.4 1.3 collective-permute-start.10
  61.7 1.3 collective-permute-start.11
  63.0 1.3 collective-permute-start.12
  64.3 1.3 collective-permute-start.13
  65.6 0.2 convert_reduce_fusion.2
  65.8 2.8 %collective-permute-start.5 = (bf16[16,64,128]{2,1,0:T(8,128)(2,1)S(1)}, bf16[16,64,128]{2,1,0:T(8,128)(2,1)S(1)}, u32[]{:S(2)}, u32[]{:S(2)}) collective-permute-start(bf16[16,64,128]{2,1,0:T(8,128)(2,1)S(1)} %copy-done.12), channel_id=1, source_target_pairs={{0,1},{1,2},{2,3},{3,4},{4,5},{5,6},{6,7},{7,8},{8,9},{9,10},{10,1... | collective-permute-start | bytes 786440 | tf_op jit(solution)/shard_map/ppermute | solution.py:325
  68.6 29.3 %collective-permute-done.10 = bf16[64,128]{1,0:T(8,128)(2,1)S(1)} collective-permute-done((bf16[64,128]{1,0:T(8,128)(2,1)S(1)}, bf16[64,128]{1,0:T(8,128)(2,1)S(1)}, u32[]{:S(2)}, u32[]{:S(2)}) %collective-permute-start.10) | collective-permute-done | bytes 16416 | tf_op jit(solution)/shard_map/ppermute | solution.py:346
  97.9 1.9 collective-permute-start.6
  99.8 1.3 collective-permute-start.14
  101.1 1.3 collective-permute-start.15
  102.5 1.3 collective-permute-start.9
  103.8 0.5 multiply_add_fusion.pos_ref
  104.3 0.3 collective-permute-done.9
  104.6 0.6 add_add_fusion.shared_ref
  105.2 2.0 collective-permute-done.6
  107.2 1.3 copy-done
  108.5 3.3 %place_blocks.1 = bf16[16,64,896]{2,1,0:T(8,128)(2,1)} custom-call(s32[96]{0:T(128)} %multiply_add_fusion.pos_ref, bf16[128,64,128]{2,1,0:T(8,128)(2,1)} %bitcast.41, bf16[64,128]{1,0:T(8,128)(2,1)} %add_add_fusion.shared_ref), custom_call_target="tpu_custom_call" | custom-call | tf_op jit(solution)/shard_map/place_blocks/pallas_call | solution.py:77
  111.8 4.5 %all-to-all-start.2 = ((bf16[16,64,896]{2,1,0:T(8,128)(2,1)}), bf16[16,64,896]{2,1,0:T(8,128)(2,1)}, u32[]{:S(2)}, u32[]{:S(2)}) async-start(bf16[16,64,896]{2,1,0:T(8,128)(2,1)} %place_blocks.1), calls=%async_computation.2 | async-start | bytes 3670016 | tf_op jit(solution)/shard_map/all_to_all | solution.py:352
  116.3 1.4 fusion.6
  117.8 1.9 collective-permute-start
  119.7 3.1 %collective-permute-start.1 = (bf16[4,256,512]{2,1,0:T(8,128)(2,1)}, bf16[4,256,512]{2,1,0:T(8,128)(2,1)}, u32[]{:S(2)}, u32[]{:S(2)}) collective-permute-start(bf16[4,256,512]{2,1,0:T(8,128)(2,1)} %bitcast.5), channel_id=1, source_target_pairs={{0,33},{1,32},{2,35},{3,34},{4,37},{5,36},{6,39},{7,38},{8,41},{9,... | collective-permute-start | bytes 3145736 | tf_op jit(solution)/shard_map/ppermute | solution.py:267
  122.8 2.9 %collective-permute-start.2 = (bf16[8,256,512]{2,1,0:T(8,128)(2,1)S(1)}, bf16[8,256,512]{2,1,0:T(8,128)(2,1)}, u32[]{:S(2)}, u32[]{:S(2)}) collective-permute-start(bf16[8,256,512]{2,1,0:T(8,128)(2,1)S(1)} %bitcast.44), channel_id=1, source_target_pairs={{0,16},{1,17},{2,18},{3,19},{4,20},{5,21},{6,22},{7,23},{8,24},{9,... | collective-permute-start | bytes 6291464 | tf_op jit(solution)/shard_map/ppermute | solution.py:267
  125.7 0.3 reduce-window.9
  126.0 0.1 slice.31
  126.1 0.1 slice_reduce_fusion
  126.2 0.1 add_bitcast_fusion
  126.3 0.4 convert_reduce_fusion
  126.7 32.9 %collective-permute-done.refs_1_ = bf16[4,256,512]{2,1,0:T(8,128)(2,1)} collective-permute-done((bf16[4,256,512]{2,1,0:T(8,128)(2,1)}, bf16[4,256,512]{2,1,0:T(8,128)(2,1)}, u32[]{:S(2)}, u32[]{:S(2)}) %collective-permute-start) | collective-permute-done | bytes 1048608 | tf_op jit(solution)/shard_map/ppermute | solution.py:267
  159.6 5.0 %collective-permute-start.3 = (bf16[4,256,512]{2,1,0:T(8,128)(2,1)}, bf16[4,256,512]{2,1,0:T(8,128)(2,1)}, u32[]{:S(2)}, u32[]{:S(2)}) collective-permute-start(bf16[4,256,512]{2,1,0:T(8,128)(2,1)} %collective-permute-done.refs_1_), channel_id=1, source_target_pairs={{0,16},{1,17},{2,18},{3,19},{4,20},{5,21},{6,22},{7,23},{8,24},{9,... | collective-permute-start | bytes 3145736 | tf_op jit(solution)/shard_map/ppermute | solution.py:267
  164.7 2.1 collective-permute-start.4
  166.8 0.2 compare_select_fusion
  167.0 0.8 pad_maximum_fusion.1.mask_ref
  167.8 1.1 pad_maximum_fusion
  168.9 0.7 collective-permute-done.4.refs_5_
  169.6 6.9 %assemble.1 = (bf16[16,64,1024]{2,1,0:T(8,128)(2,1)}, bf16[16,64,1024]{2,1,0:T(8,128)(2,1)}, bf16[16,64,1024]{2,1,0:T(8,128)(2,1)}, bf16[16,64,1024]{2,1,0:T(8,128)(2,1)}) custom-call(s32[1]{0:T(128)} %bitcast.core_ref, bf16[8,256,512]{2,1,0:T(8,128)(2,1)} %bitcast.43, bf16[4,256,512]{2,1,0:T(8,128)(2,1)} %collective-permute-done.refs_1_, ...), custom_call_target="tpu_custom_call" | custom-call | tf_op jit(solution)/shard_map/assemble/pallas_call | solution.py:252
  176.5 3.2 %fusion.2.qt_ref = bf16[1024,256]{1,0:T(8,128)(2,1)} fusion(bf16[1024,1024]{1,0:T(8,128)(2,1)} %bitcast.57, bf16[1024,256]{1,0:T(8,128)(2,1)S(1)} %bitcast.46), kind=kOutput, calls=%fused_computation.10 | convolution fusion | flops 537919488 | bytes 3145728 | tf_op jit(solution)/shard_map/dot_general | solution.py:365
  179.8 2.3 %convolution_convert_fusion.2.vt_ref = bf16[1024,512]{1,0:T(8,128)(2,1)} fusion(bf16[1024,1024]{1,0:T(8,128)(2,1)S(1)} %bitcast.56, bf16[1024,512]{1,0:T(8,128)(2,1)S(1)} %bitcast.47), kind=kOutput, calls=%fused_computation.4 | convolution fusion | flops 1074266112 | bytes 4194304 | tf_op jit(solution)/shard_map/dot_general | solution.py:368
  182.1 2.3 %convolution_convert_fusion.3.k_ref = bf16[512,1024]{1,0:T(8,128)(2,1)} fusion(bf16[1024,512]{1,0:T(8,128)(2,1)S(1)} %bitcast.48, bf16[1024,1024]{1,0:T(8,128)(2,1)S(1)} %bitcast.53), kind=kOutput, calls=%fused_computation.5 | convolution fusion | flops 1074266112 | bytes 4194304 | tf_op jit(solution)/shard_map/dot_general | solution.py:367
  184.4 8.2 %near_attention.1 = (f32[1024,256]{1,0:T(8,128)}, f32[8,2,8,256]{3,2,1,0:T(8,128)}, f32[8,2,8,256]{3,2,1,0:T(8,128)}) custom-call(bf16[1024,256]{1,0:T(8,128)(2,1)} %fusion.2.qt_ref, bf16[512,1024]{1,0:T(8,128)(2,1)} %convolution_convert_fusion.3.k_ref, bf16[1024,512]{1,0:T(8,128)(2,1)} %convolution_convert_fusion.2.vt_ref, ...), custom_call_target="tpu_custom_call" | custom-call | tf_op jit(solution)/shard_map/near_attention/pallas_call | solution.py:169
  192.6 5.7 %convolution_convert_fusion.vt_ref = bf16[1024,896]{1,0:T(8,128)(2,1)} fusion(bf16[1024,1024]{1,0:T(8,128)(2,1)} %bitcast.55, bf16[1024,896]{1,0:T(8,128)(2,1)} %bitcast.14), kind=kOutput, calls=%fused_computation.1 | convolution fusion | flops 1879965696 | bytes 5767168 | tf_op jit(solution)/shard_map/dot_general | solution.py:371
  198.3 4.9 %convolution_convert_fusion.1.k_ref = bf16[896,1024]{1,0:T(8,128)(2,1)} fusion(bf16[1024,896]{1,0:T(8,128)(2,1)} %bitcast.14, bf16[1024,1024]{1,0:T(8,128)(2,1)S(1)} %bitcast.54), kind=kOutput, calls=%fused_computation.2 | convolution fusion | flops 1879965696 | bytes 5767168 | tf_op jit(solution)/shard_map/dot_general | solution.py:370
  203.1 8.9 %far_attention.1 = bf16[1024,256]{1,0:T(8,128)(2,1)} custom-call(bf16[1024,256]{1,0:T(8,128)(2,1)} %fusion.2.qt_ref, bf16[896,1024]{1,0:T(8,128)(2,1)} %convolution_convert_fusion.1.k_ref, bf16[1024,896]{1,0:T(8,128)(2,1)} %convolution_convert_fusion.vt_ref, f32[1024,256]{1,0:T(8,128)} %get-tuple-element.29.acc_ref, ...), custom_call_target="tpu_custom_call" | custom-call | tf_op jit(solution)/shard_map/far_attention/pallas_call | solution.py:182
  212.0 2.6 %fusion.3 = bf16[256,1024]{1,0:T(8,128)(2,1)} fusion(bf16[1024,256]{1,0:T(8,128)(2,1)} %far_attention.1, bf16[1024,1024]{1,0:T(8,128)(2,1)S(1)} %bitcast.45, f32[1024]{0:T(1024)S(1)} %copy-done.6), kind=kOutput, calls=%fused_computation.11 | convolution fusion | flops 537395200 | bytes 3149824 | tf_op jit(solution)/shard_map/dot_general | solution.py:373
  (47 shorter events, 0.2 us)
Async XLA Ops:
  6.5 11.7 %copy-start.7 = (s32[1024,3]{0,1:T(4,128)S(1)}, s32[1024,3]{0,1:T(4,128)}, u32[]{:S(2)}) copy-start(s32[1024,3]{0,1:T(4,128)} %param.17) | copy-start | bytes 36868
  9.0 22.3 %all-to-all-start = ((bf16[16,64,256]{2,1,0:T(8,128)(2,1)}), bf16[16,64,256]{2,1,0:T(8,128)(2,1)S(1)}, u32[]{:S(2)}, u32[]{:S(2)}) async-start(bf16[16,64,256]{2,1,0:T(8,128)(2,1)} %get-tuple-element.20), calls=%async_computation | async-start | bytes 1048576 | tf_op jit(solution)/shard_map/all_to_all | solution.py:316
  31.3 0.8 copy-start.2
  35.7 30.0 %copy-start.12 = (bf16[16,64,128]{2,1,0:T(8,128)(2,1)S(1)}, bf16[16,64,128]{2,1,0:T(8,128)(2,1)}, u32[]{:S(2)}) copy-start(bf16[16,64,128]{2,1,0:T(8,128)(2,1)} %get-tuple-element.22) | copy-start | bytes 786436
  35.7 62.2 %copy-start.11 = (bf16[16,64,128]{2,1,0:T(8,128)(2,1)S(1)}, bf16[16,64,128]{2,1,0:T(8,128)(2,1)}, u32[]{:S(2)}) copy-start(bf16[16,64,128]{2,1,0:T(8,128)(2,1)} %get-tuple-element.24) | copy-start | bytes 786436
  35.7 71.5 %all-to-all-start.1 = ((bf16[32,256,128]{2,1,0:T(8,128)(2,1)}), bf16[32,256,128]{2,1,0:T(8,128)(2,1)S(1)}, u32[]{:S(2)}, u32[]{:S(2)}) async-start(bf16[32,256,128]{2,1,0:T(8,128)(2,1)} %bitcast.42), calls=%async_computation.1 | async-start | bytes 4194304 | tf_op jit(solution)/shard_map/all_to_all | solution.py:334
  51.1 56.1 %all-gather.3.cloned.1.call-start = ((), (), s32[]{:S(2)}) async-start(), calls=%async_computation.3 | async-start | bytes 2359296 | tf_op jit(solution)/shard_map/all_gather | solution.py:320
  52.6 0.7 collective-permute-start.7
  54.0 6.4 %collective-permute-start.8 = (bf16[64,128]{1,0:T(8,128)(2,1)S(1)}, bf16[64,128]{1,0:T(8,128)(2,1)S(1)}, u32[]{:S(2)}, u32[]{:S(2)}) collective-permute-start(bf16[64,128]{1,0:T(8,128)(2,1)S(1)} %fusion.21), channel_id=1, source_target_pairs={{0,32},{16,48},{1,33},{17,49},{2,34},{18,50},{3,35},{19,51},{4,36}... | collective-permute-start | bytes 49160 | tf_op jit(solution)/shard_map/ppermute | solution.py:344
  60.4 37.5 %collective-permute-start.10 = (bf16[64,128]{1,0:T(8,128)(2,1)S(1)}, bf16[64,128]{1,0:T(8,128)(2,1)S(1)}, u32[]{:S(2)}, u32[]{:S(2)}) collective-permute-start(bf16[64,128]{1,0:T(8,128)(2,1)S(1)} %add.64), channel_id=1, source_target_pairs={{0,128},{16,144},{32,160},{48,176},{1,129},{17,145},{33,161},{49,1... | collective-permute-start | bytes 49160 | tf_op jit(solution)/shard_map/ppermute | solution.py:346
  61.7 38.1 %collective-permute-start.11 = (bf16[64,128]{1,0:T(8,128)(2,1)S(1)}, bf16[64,128]{1,0:T(8,128)(2,1)S(1)}, u32[]{:S(2)}, u32[]{:S(2)}) collective-permute-start(bf16[64,128]{1,0:T(8,128)(2,1)S(1)} %add.64), channel_id=1, source_target_pairs={{0,192},{16,208},{32,224},{48,240},{1,193},{17,209},{33,225},{49,2... | collective-permute-start | bytes 49160 | tf_op jit(solution)/shard_map/ppermute | solution.py:346
  63.0 38.2 %collective-permute-start.12 = (bf16[64,128]{1,0:T(8,128)(2,1)S(1)}, bf16[64,128]{1,0:T(8,128)(2,1)S(1)}, u32[]{:S(2)}, u32[]{:S(2)}) collective-permute-start(bf16[64,128]{1,0:T(8,128)(2,1)S(1)} %add.64), channel_id=1, source_target_pairs={{0,256},{16,272},{32,288},{48,304},{1,257},{17,273},{33,289},{49,3... | collective-permute-start | bytes 49160 | tf_op jit(solution)/shard_map/ppermute | solution.py:346
  64.3 38.2 %collective-permute-start.13 = (bf16[64,128]{1,0:T(8,128)(2,1)S(1)}, bf16[64,128]{1,0:T(8,128)(2,1)S(1)}, u32[]{:S(2)}, u32[]{:S(2)}) collective-permute-start(bf16[64,128]{1,0:T(8,128)(2,1)S(1)} %add.64), channel_id=1, source_target_pairs={{0,320},{16,336},{32,352},{48,368},{1,321},{17,337},{33,353},{49,3... | collective-permute-start | bytes 49160 | tf_op jit(solution)/shard_map/ppermute | solution.py:346
  65.8 39.5 %collective-permute-start.5 = (bf16[16,64,128]{2,1,0:T(8,128)(2,1)S(1)}, bf16[16,64,128]{2,1,0:T(8,128)(2,1)S(1)}, u32[]{:S(2)}, u32[]{:S(2)}) collective-permute-start(bf16[16,64,128]{2,1,0:T(8,128)(2,1)S(1)} %copy-done.12), channel_id=1, source_target_pairs={{0,1},{1,2},{2,3},{3,4},{4,5},{5,6},{6,7},{7,8},{8,9},{9,10},{10,1... | collective-permute-start | bytes 786440 | tf_op jit(solution)/shard_map/ppermute | solution.py:325
  97.9 9.3 %collective-permute-start.6 = (bf16[16,64,128]{2,1,0:T(8,128)(2,1)S(1)}, bf16[16,64,128]{2,1,0:T(8,128)(2,1)S(1)}, u32[]{:S(2)}, u32[]{:S(2)}) collective-permute-start(bf16[16,64,128]{2,1,0:T(8,128)(2,1)S(1)} %copy-done.11), channel_id=1, source_target_pairs={{1,0},{2,1},{3,2},{4,3},{5,4},{6,5},{7,6},{8,7},{9,8},{10,9},{11,1... | collective-permute-start | bytes 786440 | tf_op jit(solution)/shard_map/ppermute | solution.py:326
  99.8 4.5 %collective-permute-start.14 = (bf16[64,128]{1,0:T(8,128)(2,1)S(1)}, bf16[64,128]{1,0:T(8,128)(2,1)S(1)}, u32[]{:S(2)}, u32[]{:S(2)}) collective-permute-start(bf16[64,128]{1,0:T(8,128)(2,1)S(1)} %add.64), channel_id=1, source_target_pairs={{0,384},{16,400},{32,416},{48,432},{1,385},{17,401},{33,417},{49,4... | collective-permute-start | bytes 49160 | tf_op jit(solution)/shard_map/ppermute | solution.py:346
  101.1 3.1 %collective-permute-start.15 = (bf16[64,128]{1,0:T(8,128)(2,1)S(1)}, bf16[64,128]{1,0:T(8,128)(2,1)S(1)}, u32[]{:S(2)}, u32[]{:S(2)}) collective-permute-start(bf16[64,128]{1,0:T(8,128)(2,1)S(1)} %add.64), channel_id=1, source_target_pairs={{0,448},{16,464},{32,480},{48,496},{1,449},{17,465},{33,481},{49,4... | collective-permute-start | bytes 49160 | tf_op jit(solution)/shard_map/ppermute | solution.py:346
  102.5 2.1 collective-permute-start.9
  107.2 1.3 copy-start
  111.8 4.5 %copy-start.1 = (bf16[2048,512]{1,0:T(8,128)(2,1)S(1)}, bf16[2048,512]{1,0:T(8,128)(2,1)}, u32[]{:S(2)}) copy-start(bf16[2048,512]{1,0:T(8,128)(2,1)} %all-gather.3.cloned.1.call-done) | copy-start | bytes 6291460
  111.8 80.7 %all-to-all-start.2 = ((bf16[16,64,896]{2,1,0:T(8,128)(2,1)}), bf16[16,64,896]{2,1,0:T(8,128)(2,1)}, u32[]{:S(2)}, u32[]{:S(2)}) async-start(bf16[16,64,896]{2,1,0:T(8,128)(2,1)} %place_blocks.1), calls=%async_computation.2 | async-start | bytes 3670016 | tf_op jit(solution)/shard_map/all_to_all | solution.py:352
  116.3 9.4 %copy-start.8 = (s32[1024]{0:T(1024)S(1)}, s32[1024]{0:T(1024)}, u32[]{:S(2)}) copy-start(s32[1024]{0:T(1024)} %param.15) | copy-start | bytes 12292
  116.3 51.5 %copy-start.4 = (bf16[16,64,256]{2,1,0:T(8,128)(2,1)S(1)}, bf16[16,64,256]{2,1,0:T(8,128)(2,1)}, u32[]{:S(2)}) copy-start(bf16[16,64,256]{2,1,0:T(8,128)(2,1)} %get-tuple-element.20) | copy-start | bytes 1572868
  117.8 41.8 %collective-permute-start = (bf16[4,256,512]{2,1,0:T(8,128)(2,1)}, bf16[4,256,512]{2,1,0:T(8,128)(2,1)}, u32[]{:S(2)}, u32[]{:S(2)}) collective-permute-start(bf16[4,256,512]{2,1,0:T(8,128)(2,1)} %bitcast.4), channel_id=1, source_target_pairs={{0,1},{1,0},{2,3},{3,2},{4,5},{5,4},{6,7},{7,6},{8,9},{9,8},{10,11... | collective-permute-start | bytes 3145736 | tf_op jit(solution)/shard_map/ppermute | solution.py:267
  119.7 45.0 %collective-permute-start.1 = (bf16[4,256,512]{2,1,0:T(8,128)(2,1)}, bf16[4,256,512]{2,1,0:T(8,128)(2,1)}, u32[]{:S(2)}, u32[]{:S(2)}) collective-permute-start(bf16[4,256,512]{2,1,0:T(8,128)(2,1)} %bitcast.5), channel_id=1, source_target_pairs={{0,33},{1,32},{2,35},{3,34},{4,37},{5,36},{6,39},{7,38},{8,41},{9,... | collective-permute-start | bytes 3145736 | tf_op jit(solution)/shard_map/ppermute | solution.py:267
  122.8 46.7 %collective-permute-start.2 = (bf16[8,256,512]{2,1,0:T(8,128)(2,1)S(1)}, bf16[8,256,512]{2,1,0:T(8,128)(2,1)}, u32[]{:S(2)}, u32[]{:S(2)}) collective-permute-start(bf16[8,256,512]{2,1,0:T(8,128)(2,1)S(1)} %bitcast.44), channel_id=1, source_target_pairs={{0,16},{1,17},{2,18},{3,19},{4,20},{5,21},{6,22},{7,23},{8,24},{9,... | collective-permute-start | bytes 6291464 | tf_op jit(solution)/shard_map/ppermute | solution.py:267
  159.6 9.3 %collective-permute-start.3 = (bf16[4,256,512]{2,1,0:T(8,128)(2,1)}, bf16[4,256,512]{2,1,0:T(8,128)(2,1)}, u32[]{:S(2)}, u32[]{:S(2)}) collective-permute-start(bf16[4,256,512]{2,1,0:T(8,128)(2,1)} %collective-permute-done.refs_1_), channel_id=1, source_target_pairs={{0,16},{1,17},{2,18},{3,19},{4,20},{5,21},{6,22},{7,23},{8,24},{9,... | collective-permute-start | bytes 3145736 | tf_op jit(solution)/shard_map/ppermute | solution.py:267
  164.7 4.9 %collective-permute-start.4 = (bf16[4,256,512]{2,1,0:T(8,128)(2,1)}, bf16[4,256,512]{2,1,0:T(8,128)(2,1)}, u32[]{:S(2)}, u32[]{:S(2)}) collective-permute-start(bf16[4,256,512]{2,1,0:T(8,128)(2,1)} %collective-permute-done.1.refs_2_), channel_id=1, source_target_pairs={{0,16},{1,17},{2,18},{3,19},{4,20},{5,21},{6,22},{7,23},{8,24},{9,... | collective-permute-start | bytes 3145736 | tf_op jit(solution)/shard_map/ppermute | solution.py:267
  176.5 3.3 %copy-start.5 = (bf16[16,64,512]{2,1,0:T(8,128)(2,1)S(1)}, bf16[16,64,512]{2,1,0:T(8,128)(2,1)}, u32[]{:S(2)}) copy-start(bf16[16,64,512]{2,1,0:T(8,128)(2,1)} %pad_maximum_fusion) | copy-start | bytes 3145732
  176.5 3.3 %copy-start.10 = (bf16[16,64,1024]{2,1,0:T(8,128)(2,1)S(1)}, bf16[16,64,1024]{2,1,0:T(8,128)(2,1)}, u32[]{:S(2)}) copy-start(bf16[16,64,1024]{2,1,0:T(8,128)(2,1)} %get-tuple-element.28) | copy-start | bytes 6291460
  179.8 2.3 %copy-start.9 = (bf16[16,64,1024]{2,1,0:T(8,128)(2,1)S(1)}, bf16[16,64,1024]{2,1,0:T(8,128)(2,1)}, u32[]{:S(2)}) copy-start(bf16[16,64,1024]{2,1,0:T(8,128)(2,1)} %get-tuple-element.27) | copy-start | bytes 6291460
  203.1 8.9 %copy-start.3 = (bf16[16,64,1024]{2,1,0:T(8,128)(2,1)S(1)}, bf16[16,64,1024]{2,1,0:T(8,128)(2,1)}, u32[]{:S(2)}) copy-start(bf16[16,64,1024]{2,1,0:T(8,128)(2,1)} %get-tuple-element.32) | copy-start | bytes 6291460
  203.1 8.9 %copy-start.6 = (f32[1024]{0:T(1024)S(1)}, f32[1024]{0:T(1024)}, u32[]{:S(2)}) copy-start(f32[1024]{0:T(1024)} %param.14) | copy-start | bytes 12292
Sparse Core Ops, SparseCore 0:
  54.0 41.6 all-gather.2

commit v2 on v1

--- a/solution.py
+++ b/solution.py
@@ -12,6 +12,7 @@
 EPS = 1e-05
 NEG = float("-inf")
 TN = (((0,), (1,)), ((), ()))
+BOTH_FIRST = (((0,), (0,)), ((), ()))
 
 
 def ln_kernel(tok_ref, gain_ref, bias_ref, normt_ref, first_ref, last_ref):
@@ -125,16 +126,19 @@
         sum_ref[0, b] = jnp.broadcast_to(total, sum_ref.shape[2:])
 
 
-def far_kernel(qt_ref, k_ref, vt_ref, acc_ref, top_ref, sum_ref, out_ref):
+def far_kernel(qt_ref, wk_ref, wv_ref, x_ref, acc_ref, top_ref, sum_ref, out_ref):
     f32 = jnp.float32
+    kt = jnp.dot(wk_ref[...], x_ref[...], preferred_element_type=f32).astype(jnp.bfloat16)
+    vt = jnp.dot(wv_ref[...], x_ref[...], preferred_element_type=f32).astype(jnp.bfloat16)
     spread = RAND * BLK
     shared = slice(2 * spread, 2 * spread + BLK)
     scores = []
     for b in range(2):
         q = both_heads(qt_ref[:, b * BLK : (b + 1) * BLK])
-        keys = k_ref[b * spread : (b + 1) * spread, :]
-        s = jnp.dot(keys, q, preferred_element_type=f32)
-        scores.append((s, jnp.dot(k_ref[shared, :], q, preferred_element_type=f32)))
+        keys = kt[:, b * spread : (b + 1) * spread]
+        s = lax.dot_general(keys, q, BOTH_FIRST, preferred_element_type=f32)
+        g = lax.dot_general(kt[:, shared], q, BOTH_FIRST, preferred_element_type=f32)
+        scores.append((s, g))
     for b, (s, g) in enumerate(scores):
         cols = slice(b * BLK, (b + 1) * BLK)
         far = slice(b * spread, (b + 1) * spread)
@@ -146,8 +150,8 @@
         scale = jnp.exp(old_top - top)
         total = jnp.sum(p, axis=0, keepdims=True) + sum_ref[0, b, :1] * scale
         total += jnp.sum(pg, axis=0, keepdims=True)
-        acc = jnp.dot(vt_ref[:, far], p.astype(jnp.bfloat16), preferred_element_type=f32)
-        acc += jnp.dot(vt_ref[:, shared], pg.astype(jnp.bfloat16), preferred_element_type=f32)
+        acc = jnp.dot(vt[:, far], p.astype(jnp.bfloat16), preferred_element_type=f32)
+        acc += jnp.dot(vt[:, shared], pg.astype(jnp.bfloat16), preferred_element_type=f32)
         half = acc.shape[0] // 2
         acc = own_halves(acc) + acc_ref[:, cols] * spread_rows(scale, half)
         out_ref[:, cols] = (acc / spread_rows(total, half)).astype(jnp.bfloat16)
@@ -176,17 +180,19 @@
     )(qt, k, vt, mask)
 
 
-def far_attention(qt, k, vt, parts):
+def far_attention(qt, w_k, w_v, x, parts):
     width, rows = qt.shape
-    tall, k_spec, vt_spec, row = pair_specs(rows, k.shape[0])
+    tall, _, _, row = pair_specs(rows, x.shape[1])
+    weight = pl.BlockSpec((BLK, width), lambda i: (i, 0))
+    whole = pl.BlockSpec(x.shape, lambda i: (0, 0))
     return pl.pallas_call(
         far_kernel,
         out_shape=jax.ShapeDtypeStruct((width, rows), jnp.bfloat16),
         grid=(width // BLK,),
-        in_specs=[tall, k_spec, vt_spec, tall, row, row],
+        in_specs=[tall, weight, weight, whole, tall, row, row],
         out_specs=tall,
         name="far_attention",
-    )(qt, k, vt, *parts)
+    )(qt, w_k, w_v, x, *parts)
 
 
 def run_copies(copies):
@@ -367,9 +373,7 @@
     k_near = lax.dot_general(near, w_k, TN, preferred_element_type=f32).astype(bf16)
     vt_near = jnp.dot(w_v, near, preferred_element_type=f32).astype(bf16)
     parts = near_attention(qt, k_near, vt_near, mask)
-    k_far = lax.dot_general(far, w_k, TN, preferred_element_type=f32).astype(bf16)
-    vt_far = jnp.dot(w_v, far, preferred_element_type=f32).astype(bf16)
-    attended = far_attention(qt, k_far, vt_far, parts)
+    attended = far_attention(qt, w_k, w_v, far, parts)
     projected = lax.dot_general(
         attended, w_o, (((0,), (0,)), ((), ())), preferred_element_type=f32
     )

time: 223 us -> 216 us (0.969)
  matrix products: 21 us -> 10.4 us
  Pallas kernels: 35 us -> 39.1 us
    dot_general x2 -> x0, matrix products: 10.6 us -> none  [the longest x1 5.72 us: per_device(): vt_far = jnp.dot(w_v, far, preferred_element_type=f32).astype(bf16)]
    pallas_call x1, Pallas kernels: 8.89 us -> 13 us  [far_attention(): pl.pallas_call(far_kernel, out_shape=jax.ShapeDtypeStruct((width, rows),...]
  transfers between devices with their start and end apart: 20 -> 20, of which waited for: 7 -> 7; matrix products, arithmetic and copies ran while one was open for 8% -> 9% of each run, Pallas kernels for 8% -> 8%
where the time goes in v2:
time: 216 us; the launch traced here: 215 us
  waiting for transfers between devices  80.6 us (37%)
  starting transfers between devices  58.5 us (27%)
  Pallas kernels  39.1 us (18%)
  between operations  13.8 us (6%)
  matrix products  10.4 us (5%)
  other arithmetic  6.39 us (3%)
  local copies, waits for them, and re-layouts  6.28 us (3%)
    ppermute x5, waiting for transfers between devices, swap(): lax.ppermute(value, ('ctx', 'head'), [(i, i ^ bits) for i in range(device...  33.8 us
    ppermute x7, waiting for transfers between devices, per_device(): lax.ppermute(shared, 'ctx', [(i, i + reach) for i in range(group)])  29.6 us
    all_to_all x1, starting transfers between devices, per_device(): lax.all_to_all(outgoing, 'ctx', split_axis=0, concat_axis=0, tiled=True)  15.4 us
    ppermute x5, starting transfers between devices, swap(): lax.ppermute(value, ('ctx', 'head'), [(i, i ^ bits) for i in range(device...  14.9 us
    pallas_call x1, Pallas kernels, far_attention(): pl.pallas_call(far_kernel, out_shape=jax.ShapeDtypeStruct((width, rows),...  13 us
    all_to_all x1, waiting for transfers between devices, per_device(): lax.all_to_all(normed_t, 'head', split_axis=0, concat_axis=0, tiled=True)  9.37 us
    ppermute x7, starting transfers between devices, per_device(): lax.ppermute(shared, 'ctx', [(i, i + reach) for i in range(group)])  9.03 us
    pallas_call x1, Pallas kernels, near_attention(): pl.pallas_call(near_kernel, out_shape=(jax.ShapeDtypeStruct((width, rows)...  8.18 us
  transfers between devices with their start and end apart: 20, of which 7 were waited for; matrix products, arithmetic and copies ran while one was open for 9% of the time, Pallas kernels for 8%

profile of v2, /device:TPU:7, one launch (start us, length us, event | category | flops | bytes accessed | tf_op | source)
XLA Modules:
  0.0 214.9 jit_solution(11790466135888975074)
XLA Ops:
  6.5 2.5 %layer_norm.1 = (bf16[16,64,256]{2,1,0:T(8,128)(2,1)}, bf16[16,64,128]{2,1,0:T(8,128)(2,1)}, bf16[16,64,128]{2,1,0:T(8,128)(2,1)}) custom-call(bf16[256,1024]{1,0:T(8,128)(2,1)} %tok_ref.1, f32[1,1024]{1,0:T(1,128)} %bitcast.50, f32[1,1024]{1,0:T(1,128)} %bitcast.51), custom_call_target="tpu_custom_call" | custom-call | tf_op jit(solution)/shard_map/layer_norm/pallas_call | solution.py:31
  9.0 8.0 %all-to-all-start = ((bf16[16,64,256]{2,1,0:T(8,128)(2,1)}), bf16[16,64,256]{2,1,0:T(8,128)(2,1)S(1)}, u32[]{:S(2)}, u32[]{:S(2)}) async-start(bf16[16,64,256]{2,1,0:T(8,128)(2,1)} %get-tuple-element.20), calls=%async_computation | async-start | bytes 1048576 | tf_op jit(solution)/shard_map/all_to_all | solution.py:322
  17.0 0.9 copy.12
  17.9 0.3 reshape.194
  18.2 0.2 copy.13
  18.5 0.3 broadcast_in_dim.48
  18.8 0.6 convert_reduce_fusion.1
  19.4 0.1 select_reduce_fusion
  19.5 0.1 copy.14
  19.6 0.6 reshape.195.ids_ref
  20.3 1.6 own_piece.1
  21.9 9.4 %all-to-all-done.cells_ref = bf16[16,64,256]{2,1,0:T(8,128)(2,1)S(1)} async-done(((bf16[16,64,256]{2,1,0:T(8,128)(2,1)}), bf16[16,64,256]{2,1,0:T(8,128)(2,1)S(1)}, u32[]{:S(2)}, u32[]{:S(2)}) %all-to-all-start) | async-done | bytes 524320 | tf_op jit(solution)/shard_map/all_to_all | solution.py:322
  31.3 0.8 copy-done.2
  32.1 3.7 %pick_blocks.1 = bf16[128,64,128]{2,1,0:T(8,128)(2,1)} custom-call(s32[128]{0:T(128)} %reshape.195.ids_ref, bf16[16,64,256]{2,1,0:T(8,128)(2,1)} %copy-done.2), custom_call_target="tpu_custom_call" | custom-call | tf_op jit(solution)/shard_map/pick_blocks/pallas_call | solution.py:52
  35.7 15.4 %all-to-all-start.1 = ((bf16[32,256,128]{2,1,0:T(8,128)(2,1)}), bf16[32,256,128]{2,1,0:T(8,128)(2,1)S(1)}, u32[]{:S(2)}, u32[]{:S(2)}) async-start(bf16[32,256,128]{2,1,0:T(8,128)(2,1)} %bitcast.38), calls=%async_computation.1 | async-start | bytes 4194304 | tf_op jit(solution)/shard_map/all_to_all | solution.py:340
  51.1 0.0 all-gather.3.cloned.1.call-start
  51.2 0.7 all-gather.3.cloned.1.call-update
  51.9 0.7 fusion.5
  52.6 0.7 collective-permute-start.7
  53.3 0.7 fusion.17
  54.0 1.3 collective-permute-start.8
  55.3 5.1 %collective-permute-done.8 = bf16[64,128]{1,0:T(8,128)(2,1)S(1)} collective-permute-done((bf16[64,128]{1,0:T(8,128)(2,1)S(1)}, bf16[64,128]{1,0:T(8,128)(2,1)S(1)}, u32[]{:S(2)}, u32[]{:S(2)}) %collective-permute-start.8) | collective-permute-done | bytes 16416 | tf_op jit(solution)/shard_map/ppermute | solution.py:350
  60.4 1.3 collective-permute-start.10
  61.7 1.3 collective-permute-start.11
  63.0 1.3 collective-permute-start.12
  64.3 1.3 collective-permute-start.13
  65.6 0.2 convert_reduce_fusion.2
  65.8 2.8 %collective-permute-start.5 = (bf16[16,64,128]{2,1,0:T(8,128)(2,1)S(1)}, bf16[16,64,128]{2,1,0:T(8,128)(2,1)S(1)}, u32[]{:S(2)}, u32[]{:S(2)}) collective-permute-start(bf16[16,64,128]{2,1,0:T(8,128)(2,1)S(1)} %copy-done.12), channel_id=1, source_target_pairs={{0,1},{1,2},{2,3},{3,4},{4,5},{5,6},{6,7},{7,8},{8,9},{9,10},{10,1... | collective-permute-start | bytes 786440 | tf_op jit(solution)/shard_map/ppermute | solution.py:331
  68.6 29.3 %collective-permute-done.10 = bf16[64,128]{1,0:T(8,128)(2,1)S(1)} collective-permute-done((bf16[64,128]{1,0:T(8,128)(2,1)S(1)}, bf16[64,128]{1,0:T(8,128)(2,1)S(1)}, u32[]{:S(2)}, u32[]{:S(2)}) %collective-permute-start.10) | collective-permute-done | bytes 16416 | tf_op jit(solution)/shard_map/ppermute | solution.py:352
  97.9 1.9 collective-permute-start.6
  99.8 1.3 collective-permute-start.14
  101.1 1.3 collective-permute-start.15
  102.5 1.3 collective-permute-start.9
  103.8 0.5 multiply_add_fusion.pos_ref
  104.3 0.3 collective-permute-done.9
  104.6 0.6 add_add_fusion.shared_ref
  105.2 2.0 collective-permute-done.6
  107.2 1.3 copy-done
  108.5 3.3 %place_blocks.1 = bf16[16,64,896]{2,1,0:T(8,128)(2,1)} custom-call(s32[96]{0:T(128)} %multiply_add_fusion.pos_ref, bf16[128,64,128]{2,1,0:T(8,128)(2,1)} %bitcast.37, bf16[64,128]{1,0:T(8,128)(2,1)} %add_add_fusion.shared_ref), custom_call_target="tpu_custom_call" | custom-call | tf_op jit(solution)/shard_map/place_blocks/pallas_call | solution.py:78
  111.8 4.4 %all-to-all-start.2 = ((bf16[16,64,896]{2,1,0:T(8,128)(2,1)}), bf16[16,64,896]{2,1,0:T(8,128)(2,1)}, u32[]{:S(2)}, u32[]{:S(2)}) async-start(bf16[16,64,896]{2,1,0:T(8,128)(2,1)} %place_blocks.1), calls=%async_computation.2 | async-start | bytes 3670016 | tf_op jit(solution)/shard_map/all_to_all | solution.py:358
  116.3 0.0 copy-start.4
  116.3 1.5 fusion.6
  117.8 1.9 collective-permute-start
  119.7 3.1 %collective-permute-start.1 = (bf16[4,256,512]{2,1,0:T(8,128)(2,1)}, bf16[4,256,512]{2,1,0:T(8,128)(2,1)}, u32[]{:S(2)}, u32[]{:S(2)}) collective-permute-start(bf16[4,256,512]{2,1,0:T(8,128)(2,1)} %bitcast.5), channel_id=1, source_target_pairs={{0,33},{1,32},{2,35},{3,34},{4,37},{5,36},{6,39},{7,38},{8,41},{9,... | collective-permute-start | bytes 3145736 | tf_op jit(solution)/shard_map/ppermute | solution.py:273
  122.9 2.9 %collective-permute-start.2 = (bf16[8,256,512]{2,1,0:T(8,128)(2,1)S(1)}, bf16[8,256,512]{2,1,0:T(8,128)(2,1)}, u32[]{:S(2)}, u32[]{:S(2)}) collective-permute-start(bf16[8,256,512]{2,1,0:T(8,128)(2,1)S(1)} %bitcast.40), channel_id=1, source_target_pairs={{0,16},{1,17},{2,18},{3,19},{4,20},{5,21},{6,22},{7,23},{8,24},{9,... | collective-permute-start | bytes 6291464 | tf_op jit(solution)/shard_map/ppermute | solution.py:273
  125.7 0.3 reduce-window.9
  126.0 0.1 slice.31
  126.1 0.1 slice_reduce_fusion
  126.2 0.1 add_bitcast_fusion
  126.3 0.4 convert_reduce_fusion
  126.7 33.0 %collective-permute-done.refs_1_ = bf16[4,256,512]{2,1,0:T(8,128)(2,1)} collective-permute-done((bf16[4,256,512]{2,1,0:T(8,128)(2,1)}, bf16[4,256,512]{2,1,0:T(8,128)(2,1)}, u32[]{:S(2)}, u32[]{:S(2)}) %collective-permute-start) | collective-permute-done | bytes 1048608 | tf_op jit(solution)/shard_map/ppermute | solution.py:273
  159.6 5.0 %collective-permute-start.3 = (bf16[4,256,512]{2,1,0:T(8,128)(2,1)}, bf16[4,256,512]{2,1,0:T(8,128)(2,1)}, u32[]{:S(2)}, u32[]{:S(2)}) collective-permute-start(bf16[4,256,512]{2,1,0:T(8,128)(2,1)} %collective-permute-done.refs_1_), channel_id=1, source_target_pairs={{0,16},{1,17},{2,18},{3,19},{4,20},{5,21},{6,22},{7,23},{8,24},{9,... | collective-permute-start | bytes 3145736 | tf_op jit(solution)/shard_map/ppermute | solution.py:273
  164.7 1.9 collective-permute-start.4
  166.6 0.2 compare_select_fusion
  166.8 0.8 pad_maximum_fusion.1.mask_ref
  167.6 1.1 pad_maximum_fusion
  168.7 0.8 collective-permute-done.4.refs_5_
  169.6 6.9 %assemble.1 = (bf16[16,64,1024]{2,1,0:T(8,128)(2,1)}, bf16[16,64,1024]{2,1,0:T(8,128)(2,1)}, bf16[16,64,1024]{2,1,0:T(8,128)(2,1)}, bf16[16,64,1024]{2,1,0:T(8,128)(2,1)}) custom-call(s32[1]{0:T(128)} %bitcast.core_ref, bf16[8,256,512]{2,1,0:T(8,128)(2,1)} %bitcast.39, bf16[4,256,512]{2,1,0:T(8,128)(2,1)} %collective-permute-done.refs_1_, ...), custom_call_target="tpu_custom_call" | custom-call | tf_op jit(solution)/shard_map/assemble/pallas_call | solution.py:258
  176.5 3.2 %fusion.2.qt_ref = bf16[1024,256]{1,0:T(8,128)(2,1)} fusion(bf16[1024,1024]{1,0:T(8,128)(2,1)} %bitcast.53, bf16[1024,256]{1,0:T(8,128)(2,1)S(1)} %bitcast.42), kind=kOutput, calls=%fused_computation.8 | convolution fusion | flops 537919488 | bytes 3145728 | tf_op jit(solution)/shard_map/dot_general | solution.py:371
  179.7 2.3 %convolution_convert_fusion.vt_ref = bf16[1024,512]{1,0:T(8,128)(2,1)} fusion(bf16[1024,1024]{1,0:T(8,128)(2,1)S(1)} %bitcast.46, bf16[1024,512]{1,0:T(8,128)(2,1)S(1)} %bitcast.47), kind=kOutput, calls=%fused_computation.2 | convolution fusion | flops 1074266112 | bytes 4194304 | tf_op jit(solution)/shard_map/dot_general | solution.py:374
  182.0 2.3 %convolution_convert_fusion.1.k_ref = bf16[512,1024]{1,0:T(8,128)(2,1)} fusion(bf16[1024,512]{1,0:T(8,128)(2,1)S(1)} %bitcast.48, bf16[1024,1024]{1,0:T(8,128)(2,1)S(1)} %bitcast.44), kind=kOutput, calls=%fused_computation.3 | convolution fusion | flops 1074266112 | bytes 4194304 | tf_op jit(solution)/shard_map/dot_general | solution.py:373
  184.3 8.2 %near_attention.1 = (f32[1024,256]{1,0:T(8,128)}, f32[8,2,8,256]{3,2,1,0:T(8,128)}, f32[8,2,8,256]{3,2,1,0:T(8,128)}) custom-call(bf16[1024,256]{1,0:T(8,128)(2,1)} %fusion.2.qt_ref, bf16[512,1024]{1,0:T(8,128)(2,1)} %convolution_convert_fusion.1.k_ref, bf16[1024,512]{1,0:T(8,128)(2,1)} %convolution_convert_fusion.vt_ref, ...), custom_call_target="tpu_custom_call" | custom-call | tf_op jit(solution)/shard_map/near_attention/pallas_call | solution.py:173
  192.5 13.0 %far_attention.1 = bf16[1024,256]{1,0:T(8,128)(2,1)} custom-call(bf16[1024,256]{1,0:T(8,128)(2,1)} %fusion.2.qt_ref, bf16[1024,1024]{1,0:T(8,128)(2,1)} %bitcast.43, bf16[1024,1024]{1,0:T(8,128)(2,1)} %bitcast.45, bf16[1024,896]{1,0:T(8,128)(2,1)} %bitcast.16.x_ref, f32[1024,256]{1,0:T(8,128)} %get-tuple-element.29.acc_ref, ...), custom_call_target="tpu_custom_call" | custom-call | tf_op jit(solution)/shard_map/far_attention/pallas_call | solution.py:188
  205.5 2.6 %fusion.3 = bf16[256,1024]{1,0:T(8,128)(2,1)} fusion(bf16[1024,256]{1,0:T(8,128)(2,1)} %far_attention.1, bf16[1024,1024]{1,0:T(8,128)(2,1)S(1)} %bitcast.41, f32[1024]{0:T(1024)S(1)} %copy-done.8), kind=kOutput, calls=%fused_computation.9 | convolution fusion | flops 537395200 | bytes 3149824 | tf_op jit(solution)/shard_map/dot_general | solution.py:377
  (45 shorter events, 0.2 us)
Async XLA Ops:
  6.5 11.7 %copy-start.9 = (s32[1024,3]{0,1:T(4,128)S(1)}, s32[1024,3]{0,1:T(4,128)}, u32[]{:S(2)}) copy-start(s32[1024,3]{0,1:T(4,128)} %param.17) | copy-start | bytes 36868
  9.0 22.3 %all-to-all-start = ((bf16[16,64,256]{2,1,0:T(8,128)(2,1)}), bf16[16,64,256]{2,1,0:T(8,128)(2,1)S(1)}, u32[]{:S(2)}, u32[]{:S(2)}) async-start(bf16[16,64,256]{2,1,0:T(8,128)(2,1)} %get-tuple-element.20), calls=%async_computation | async-start | bytes 1048576 | tf_op jit(solution)/shard_map/all_to_all | solution.py:322
  31.3 0.8 copy-start.2
  35.7 30.0 %copy-start.12 = (bf16[16,64,128]{2,1,0:T(8,128)(2,1)S(1)}, bf16[16,64,128]{2,1,0:T(8,128)(2,1)}, u32[]{:S(2)}) copy-start(bf16[16,64,128]{2,1,0:T(8,128)(2,1)} %get-tuple-element.24) | copy-start | bytes 786436
  35.7 62.2 %copy-start.11 = (bf16[16,64,128]{2,1,0:T(8,128)(2,1)S(1)}, bf16[16,64,128]{2,1,0:T(8,128)(2,1)}, u32[]{:S(2)}) copy-start(bf16[16,64,128]{2,1,0:T(8,128)(2,1)} %get-tuple-element.26) | copy-start | bytes 786436
  35.7 71.5 %all-to-all-start.1 = ((bf16[32,256,128]{2,1,0:T(8,128)(2,1)}), bf16[32,256,128]{2,1,0:T(8,128)(2,1)S(1)}, u32[]{:S(2)}, u32[]{:S(2)}) async-start(bf16[32,256,128]{2,1,0:T(8,128)(2,1)} %bitcast.38), calls=%async_computation.1 | async-start | bytes 4194304 | tf_op jit(solution)/shard_map/all_to_all | solution.py:340
  51.1 56.1 %all-gather.3.cloned.1.call-start = ((), (), s32[]{:S(2)}) async-start(), calls=%async_computation.3 | async-start | bytes 2359296 | tf_op jit(solution)/shard_map/all_gather | solution.py:326
  52.6 0.7 collective-permute-start.7
  54.0 6.4 %collective-permute-start.8 = (bf16[64,128]{1,0:T(8,128)(2,1)S(1)}, bf16[64,128]{1,0:T(8,128)(2,1)S(1)}, u32[]{:S(2)}, u32[]{:S(2)}) collective-permute-start(bf16[64,128]{1,0:T(8,128)(2,1)S(1)} %fusion.17), channel_id=1, source_target_pairs={{0,32},{16,48},{1,33},{17,49},{2,34},{18,50},{3,35},{19,51},{4,36}... | collective-permute-start | bytes 49160 | tf_op jit(solution)/shard_map/ppermute | solution.py:350
  60.4 37.5 %collective-permute-start.10 = (bf16[64,128]{1,0:T(8,128)(2,1)S(1)}, bf16[64,128]{1,0:T(8,128)(2,1)S(1)}, u32[]{:S(2)}, u32[]{:S(2)}) collective-permute-start(bf16[64,128]{1,0:T(8,128)(2,1)S(1)} %add.64), channel_id=1, source_target_pairs={{0,128},{16,144},{32,160},{48,176},{1,129},{17,145},{33,161},{49,1... | collective-permute-start | bytes 49160 | tf_op jit(solution)/shard_map/ppermute | solution.py:352
  61.7 38.1 %collective-permute-start.11 = (bf16[64,128]{1,0:T(8,128)(2,1)S(1)}, bf16[64,128]{1,0:T(8,128)(2,1)S(1)}, u32[]{:S(2)}, u32[]{:S(2)}) collective-permute-start(bf16[64,128]{1,0:T(8,128)(2,1)S(1)} %add.64), channel_id=1, source_target_pairs={{0,192},{16,208},{32,224},{48,240},{1,193},{17,209},{33,225},{49,2... | collective-permute-start | bytes 49160 | tf_op jit(solution)/shard_map/ppermute | solution.py:352
  63.0 38.2 %collective-permute-start.12 = (bf16[64,128]{1,0:T(8,128)(2,1)S(1)}, bf16[64,128]{1,0:T(8,128)(2,1)S(1)}, u32[]{:S(2)}, u32[]{:S(2)}) collective-permute-start(bf16[64,128]{1,0:T(8,128)(2,1)S(1)} %add.64), channel_id=1, source_target_pairs={{0,256},{16,272},{32,288},{48,304},{1,257},{17,273},{33,289},{49,3... | collective-permute-start | bytes 49160 | tf_op jit(solution)/shard_map/ppermute | solution.py:352
  64.3 38.2 %collective-permute-start.13 = (bf16[64,128]{1,0:T(8,128)(2,1)S(1)}, bf16[64,128]{1,0:T(8,128)(2,1)S(1)}, u32[]{:S(2)}, u32[]{:S(2)}) collective-permute-start(bf16[64,128]{1,0:T(8,128)(2,1)S(1)} %add.64), channel_id=1, source_target_pairs={{0,320},{16,336},{32,352},{48,368},{1,321},{17,337},{33,353},{49,3... | collective-permute-start | bytes 49160 | tf_op jit(solution)/shard_map/ppermute | solution.py:352
  65.8 39.5 %collective-permute-start.5 = (bf16[16,64,128]{2,1,0:T(8,128)(2,1)S(1)}, bf16[16,64,128]{2,1,0:T(8,128)(2,1)S(1)}, u32[]{:S(2)}, u32[]{:S(2)}) collective-permute-start(bf16[16,64,128]{2,1,0:T(8,128)(2,1)S(1)} %copy-done.12), channel_id=1, source_target_pairs={{0,1},{1,2},{2,3},{3,4},{4,5},{5,6},{6,7},{7,8},{8,9},{9,10},{10,1... | collective-permute-start | bytes 786440 | tf_op jit(solution)/shard_map/ppermute | solution.py:331
  97.9 9.3 %collective-permute-start.6 = (bf16[16,64,128]{2,1,0:T(8,128)(2,1)S(1)}, bf16[16,64,128]{2,1,0:T(8,128)(2,1)S(1)}, u32[]{:S(2)}, u32[]{:S(2)}) collective-permute-start(bf16[16,64,128]{2,1,0:T(8,128)(2,1)S(1)} %copy-done.11), channel_id=1, source_target_pairs={{1,0},{2,1},{3,2},{4,3},{5,4},{6,5},{7,6},{8,7},{9,8},{10,9},{11,1... | collective-permute-start | bytes 786440 | tf_op jit(solution)/shard_map/ppermute | solution.py:332
  99.8 4.5 %collective-permute-start.14 = (bf16[64,128]{1,0:T(8,128)(2,1)S(1)}, bf16[64,128]{1,0:T(8,128)(2,1)S(1)}, u32[]{:S(2)}, u32[]{:S(2)}) collective-permute-start(bf16[64,128]{1,0:T(8,128)(2,1)S(1)} %add.64), channel_id=1, source_target_pairs={{0,384},{16,400},{32,416},{48,432},{1,385},{17,401},{33,417},{49,4... | collective-permute-start | bytes 49160 | tf_op jit(solution)/shard_map/ppermute | solution.py:352
  101.1 3.1 %collective-permute-start.15 = (bf16[64,128]{1,0:T(8,128)(2,1)S(1)}, bf16[64,128]{1,0:T(8,128)(2,1)S(1)}, u32[]{:S(2)}, u32[]{:S(2)}) collective-permute-start(bf16[64,128]{1,0:T(8,128)(2,1)S(1)} %add.64), channel_id=1, source_target_pairs={{0,448},{16,464},{32,480},{48,496},{1,449},{17,465},{33,481},{49,4... | collective-permute-start | bytes 49160 | tf_op jit(solution)/shard_map/ppermute | solution.py:352
  102.5 2.1 %collective-permute-start.9 = (bf16[64,128]{1,0:T(8,128)(2,1)S(1)}, bf16[64,128]{1,0:T(8,128)(2,1)S(1)}, u32[]{:S(2)}, u32[]{:S(2)}) collective-permute-start(bf16[64,128]{1,0:T(8,128)(2,1)S(1)} %add.64), channel_id=1, source_target_pairs={{0,64},{16,80},{32,96},{48,112},{1,65},{17,81},{33,97},{49,113},{2... | collective-permute-start | bytes 49160 | tf_op jit(solution)/shard_map/ppermute | solution.py:352
  107.2 1.3 copy-start
  111.8 4.5 %copy-start.1 = (bf16[2048,512]{1,0:T(8,128)(2,1)S(1)}, bf16[2048,512]{1,0:T(8,128)(2,1)}, u32[]{:S(2)}) copy-start(bf16[2048,512]{1,0:T(8,128)(2,1)} %all-gather.3.cloned.1.call-done) | copy-start | bytes 6291460
  111.8 80.7 %all-to-all-start.2 = ((bf16[16,64,896]{2,1,0:T(8,128)(2,1)}), bf16[16,64,896]{2,1,0:T(8,128)(2,1)}, u32[]{:S(2)}, u32[]{:S(2)}) async-start(bf16[16,64,896]{2,1,0:T(8,128)(2,1)} %place_blocks.1), calls=%async_computation.2 | async-start | bytes 3670016 | tf_op jit(solution)/shard_map/all_to_all | solution.py:358
  116.3 9.5 %copy-start.10 = (s32[1024]{0:T(1024)S(1)}, s32[1024]{0:T(1024)}, u32[]{:S(2)}) copy-start(s32[1024]{0:T(1024)} %param.15) | copy-start | bytes 12292
  116.3 51.3 %copy-start.4 = (bf16[16,64,256]{2,1,0:T(8,128)(2,1)S(1)}, bf16[16,64,256]{2,1,0:T(8,128)(2,1)}, u32[]{:S(2)}) copy-start(bf16[16,64,256]{2,1,0:T(8,128)(2,1)} %get-tuple-element.20) | copy-start | bytes 1572868
  117.8 41.8 %collective-permute-start = (bf16[4,256,512]{2,1,0:T(8,128)(2,1)}, bf16[4,256,512]{2,1,0:T(8,128)(2,1)}, u32[]{:S(2)}, u32[]{:S(2)}) collective-permute-start(bf16[4,256,512]{2,1,0:T(8,128)(2,1)} %bitcast.4), channel_id=1, source_target_pairs={{0,1},{1,0},{2,3},{3,2},{4,5},{5,4},{6,7},{7,6},{8,9},{9,8},{10,11... | collective-permute-start | bytes 3145736 | tf_op jit(solution)/shard_map/ppermute | solution.py:273
  119.7 45.0 %collective-permute-start.1 = (bf16[4,256,512]{2,1,0:T(8,128)(2,1)}, bf16[4,256,512]{2,1,0:T(8,128)(2,1)}, u32[]{:S(2)}, u32[]{:S(2)}) collective-permute-start(bf16[4,256,512]{2,1,0:T(8,128)(2,1)} %bitcast.5), channel_id=1, source_target_pairs={{0,33},{1,32},{2,35},{3,34},{4,37},{5,36},{6,39},{7,38},{8,41},{9,... | collective-permute-start | bytes 3145736 | tf_op jit(solution)/shard_map/ppermute | solution.py:273
  122.9 46.7 %collective-permute-start.2 = (bf16[8,256,512]{2,1,0:T(8,128)(2,1)S(1)}, bf16[8,256,512]{2,1,0:T(8,128)(2,1)}, u32[]{:S(2)}, u32[]{:S(2)}) collective-permute-start(bf16[8,256,512]{2,1,0:T(8,128)(2,1)S(1)} %bitcast.40), channel_id=1, source_target_pairs={{0,16},{1,17},{2,18},{3,19},{4,20},{5,21},{6,22},{7,23},{8,24},{9,... | collective-permute-start | bytes 6291464 | tf_op jit(solution)/shard_map/ppermute | solution.py:273
  159.6 9.1 %collective-permute-start.3 = (bf16[4,256,512]{2,1,0:T(8,128)(2,1)}, bf16[4,256,512]{2,1,0:T(8,128)(2,1)}, u32[]{:S(2)}, u32[]{:S(2)}) collective-permute-start(bf16[4,256,512]{2,1,0:T(8,128)(2,1)} %collective-permute-done.refs_1_), channel_id=1, source_target_pairs={{0,16},{1,17},{2,18},{3,19},{4,20},{5,21},{6,22},{7,23},{8,24},{9,... | collective-permute-start | bytes 3145736 | tf_op jit(solution)/shard_map/ppermute | solution.py:273
  164.7 4.9 %collective-permute-start.4 = (bf16[4,256,512]{2,1,0:T(8,128)(2,1)}, bf16[4,256,512]{2,1,0:T(8,128)(2,1)}, u32[]{:S(2)}, u32[]{:S(2)}) collective-permute-start(bf16[4,256,512]{2,1,0:T(8,128)(2,1)} %collective-permute-done.1.refs_2_), channel_id=1, source_target_pairs={{0,16},{1,17},{2,18},{3,19},{4,20},{5,21},{6,22},{7,23},{8,24},{9,... | collective-permute-start | bytes 3145736 | tf_op jit(solution)/shard_map/ppermute | solution.py:273
  176.5 3.3 %copy-start.6 = (bf16[16,64,1024]{2,1,0:T(8,128)(2,1)S(1)}, bf16[16,64,1024]{2,1,0:T(8,128)(2,1)}, u32[]{:S(2)}) copy-start(bf16[16,64,1024]{2,1,0:T(8,128)(2,1)} %get-tuple-element.22) | copy-start | bytes 6291460
  176.5 3.3 %copy-start.7 = (bf16[16,64,512]{2,1,0:T(8,128)(2,1)S(1)}, bf16[16,64,512]{2,1,0:T(8,128)(2,1)}, u32[]{:S(2)}) copy-start(bf16[16,64,512]{2,1,0:T(8,128)(2,1)} %pad_maximum_fusion) | copy-start | bytes 3145732
  179.7 2.3 %copy-start.5 = (bf16[16,64,1024]{2,1,0:T(8,128)(2,1)S(1)}, bf16[16,64,1024]{2,1,0:T(8,128)(2,1)}, u32[]{:S(2)}) copy-start(bf16[16,64,1024]{2,1,0:T(8,128)(2,1)} %get-tuple-element.21) | copy-start | bytes 6291460
  192.5 13.0 %copy-start.3 = (bf16[16,64,1024]{2,1,0:T(8,128)(2,1)S(1)}, bf16[16,64,1024]{2,1,0:T(8,128)(2,1)}, u32[]{:S(2)}) copy-start(bf16[16,64,1024]{2,1,0:T(8,128)(2,1)} %get-tuple-element.32) | copy-start | bytes 6291460
  192.5 13.0 %copy-start.8 = (f32[1024]{0:T(1024)S(1)}, f32[1024]{0:T(1024)}, u32[]{:S(2)}) copy-start(f32[1024]{0:T(1024)} %param.14) | copy-start | bytes 12292
Sparse Core Ops, SparseCore 0:
  54.0 41.6 all-gather.2
